TPU v7x, 256 devices: a whole 4x4x8 slice. The times are simulated.
256 devices in a mesh: row: 8 (over x, z_hi), col: 32 (over y, z_lo, core).
Axes of the slice: x: 4, y: 4, z: 8 (z_hi: 2, z_lo: 4; z = z_hi * 4 + z_lo), core: 2. Of those that a mesh axis runs over, the one named last changes fastest.
Arguments:
- matrix: float32 [16384, 16384], P('row', 'col'), may hold values from -6 to 6, as said below
- vectors: float32 [2, 16384, 128], P(None, ('row', 'col')), may hold values from -0.16 to 0.16
- tfactor: float32 [2, 128, 128], replicated, may hold values from -0.5 to 0.5
Outputs:
- updated: float32 [16384, 16384], P('row', 'col')
Inputs may be any that keep to these rules, and one draw needn't show every extreme that they name: matrix is symmetric: matrix[i, j] equals matrix[j, i].
All inputs are finite; a program needn't handle non-finite values.
Results may differ from a plain program's by a relative error of at most 0.00012.
Values sent between devices are 32-bit elements; how exact they have to be, the bound alone decides.
A program may use at most 64 MiB of HBM per device.

v0:
```python
import jax
import jax.numpy as jnp
from jax import lax
from jax.sharding import PartitionSpec as P

highest = lax.Precision.HIGHEST


def spread(block, axis, source):
    block = jnp.where(lax.axis_index(axis) == source, block, jnp.zeros_like(block))
    return lax.psum(block, axis)


def mat_product(left, right):
    return jnp.dot(left, right, precision=highest, preferred_element_type=jnp.float32)


def body(matrix, vectors, tfactor):
    rows_here, cols_here = matrix.shape
    panels = vectors.shape[0]
    own_count = vectors.shape[1]
    row_total = lax.axis_size("row")
    col_total = lax.axis_size("col")
    row_index = lax.axis_index("row")
    col_index = lax.axis_index("col")
    owner_row = col_index * row_total // col_total
    offset = col_index * cols_here - owner_row * rows_here
    v_rows = lax.all_gather(vectors, "col", axis=1, tiled=True)
    v_local = lax.dynamic_slice_in_dim(v_rows, offset, cols_here, 1)
    v_cols = spread(v_local, "row", owner_row)
    current = matrix
    for panel_index in range(panels):
        vector_i = v_rows[panel_index]
        vector_j = v_cols[panel_index]
        own_rows = vectors[panel_index]
        factor = jnp.triu(tfactor[panel_index])

        def partial_rows(begin_row, span_rows, current=current, vector_j=vector_j):
            return mat_product(current, vector_j)

        summed = lax.psum_scatter(
            partial_rows(jnp.int32(0), own_count * lax.axis_size("col")),
            "col",
            scatter_dimension=0,
            tiled=True,
        )
        ymatrix = mat_product(summed, factor)
        gram_matrix = lax.psum(mat_product(own_rows.T, ymatrix), ("row", "col"))
        w_own = ymatrix - 0.5 * mat_product(own_rows, mat_product(factor.T, gram_matrix))
        w_all = lax.all_gather(w_own, ("row", "col"), axis=0, tiled=True)
        w_i = lax.dynamic_slice_in_dim(w_all, row_index * rows_here, rows_here, 0)
        w_j = lax.dynamic_slice_in_dim(w_all, col_index * cols_here, cols_here, 0)
        current = current - mat_product(vector_i, w_j.T) - mat_product(w_i, vector_j.T)
    return current


def solution(mesh):
    return jax.shard_map(
        body,
        mesh=mesh,
        in_specs=(P("row", "col"), P(None, ("row", "col"), None), P()),
        out_specs=P("row", "col"),
        check_vma=False,
    )
```

profile of v0, /device:TPU:1, one launch (start us, length us, event | category | flops | bytes accessed | tf_op | source)
XLA Modules:
  0.0 1845.5 jit_solution(2119604143348090658)
XLA Ops:
  7.3 65.8 %all-gather.4.cloned.1.call-done = f32[2,2048,128]{2,1,0:T(8,128)} async-done(((f32[2,64,128]{2,1,0:T(8,128)}), f32[2,2048,128]{2,1,0:T(8,128)}) %all-gather.4.cloned.1.call-update) | async-done | bytes 2097168 | tf_op jit(solution)/shard_map/all_gather | solution.py:28
  73.1 1.9 dynamic-slice_select_fusion
  75.1 104.8 %all-reduce.4.cloned.1.call-done = f32[2,512,128]{2,1,0:T(8,128)} async-done(((f32[2,512,128]{2,1,0:T(8,128)}), f32[2,512,128]{2,1,0:T(8,128)}) %all-reduce.4.cloned.1.call-update) | async-done | bytes 524304 | tf_op jit(solution)/shard_map/psum | solution.py:11
  179.9 6.7 convolution_bitcast_fusion
  186.7 1.3 copy.14
  188.1 142.6 %reduce-scatter.7.cloned.1.call-done = f32[64,128]{1,0:T(8,128)} async-done(((f32[2048,128]{1,0:T(8,128)}), f32[64,128]{1,0:T(8,128)}) %reduce-scatter.7.cloned.1.call-update) | async-done | bytes 32784
  330.6 1.0 fusion.14
  331.7 0.9 convolution_bitcast_fusion.2
  332.7 246.7 %all-reduce.6.cloned.1.call-done = f32[128,128]{0,1:T(8,128)} async-done(((f32[128,128]{0,1:T(8,128)}), f32[128,128]{0,1:T(8,128)}) %all-reduce.6.cloned.1.call-update) | async-done | bytes 65552 | tf_op jit(solution)/shard_map/psum | solution.py:48
  579.3 1.2 fusion.13
  581.4 5.5 copy.8
  586.9 409.2 %all-gather.6.cloned.1.call-done = f32[16384,128]{1,0:T(8,128)} async-done(((f32[64,128]{1,0:T(8,128)}), f32[16384,128]{1,0:T(8,128)}) %all-gather.6.cloned.1.call-update) | async-done | bytes 8388624 | tf_op jit(solution)/shard_map/all_gather | solution.py:50
  996.1 4.9 fusion.8
  1001.0 4.9 fusion.1
  1006.0 2.0 copy-done
  1008.0 8.1 fusion.12
  1016.2 140.3 %reduce-scatter.5.cloned.1.call-done = f32[64,128]{1,0:T(8,128)} async-done(((f32[2048,128]{1,0:T(8,128)}), f32[64,128]{1,0:T(8,128)}) %reduce-scatter.5.cloned.1.call-update) | async-done | bytes 32784 | tf_op jit(solution)/shard_map/reduce_scatter | solution.py:41
  1156.5 1.0 fusion.16
  1158.5 246.6 %all-reduce.8.cloned.1.call-done = f32[128,128]{0,1:T(8,128)} async-done(((f32[128,128]{0,1:T(8,128)}), f32[128,128]{0,1:T(8,128)}) %all-reduce.8.cloned.1.call-update) | async-done | bytes 65552 | tf_op jit(solution)/shard_map/psum | solution.py:48
  1405.1 1.2 fusion.15
  1407.1 414.8 %all-gather.8.cloned.1.call-done = f32[16384,128]{1,0:T(8,128)} async-done(((f32[64,128]{1,0:T(8,128)}), f32[16384,128]{1,0:T(8,128)}) %all-gather.8.cloned.1.call-update) | async-done | bytes 8388624 | tf_op jit(solution)/shard_map/all_gather | solution.py:50
  1821.9 4.9 fusion.6
  1826.8 6.5 fusion
  1833.3 5.3 copy.11
  (33 shorter events, 3.7 us)
Async XLA Ops:
  6.5 66.6 %all-gather.4.cloned.1.call-start = ((), (), s32[]{:S(2)}) async-start(), calls=%async_computation.2 | async-start | bytes 2162688 | tf_op jit(solution)/shard_map/all_gather | solution.py:28
  7.3 172.7 %all-reduce.4.cloned.1.call-start = ((), (), s32[]{:S(2)}) async-start(), calls=%async_computation.3 | async-start | bytes 1048576 | tf_op jit(solution)/shard_map/psum | solution.py:11
  75.0 255.6 %copy-start.6 = (f32[2,128,128]{2,1,0:T(8,128)S(1)}, f32[2,128,128]{2,1,0:T(8,128)}, u32[]{:S(2)}) copy-start(f32[2,128,128]{2,1,0:T(8,128)} %param.5) | copy-start | bytes 393220
  75.0 256.6 %copy-start.5 = (f32[2,64,128]{2,1,0:T(8,128)S(1)}, f32[2,64,128]{2,1,0:T(8,128)}, u32[]{:S(2)}) copy-start(f32[2,64,128]{2,1,0:T(8,128)} %param.4) | copy-start | bytes 196612
  75.1 255.6 %reduce-scatter.7.cloned.1.call-start = ((), (), s32[]{:S(2)}) async-start(), calls=%async_computation.9 | async-start | bytes 1081344
  188.0 391.3 %all-reduce.6.cloned.1.call-start = ((), (), s32[]{:S(2)}) async-start(), calls=%async_computation.4 | async-start | bytes 131072 | tf_op jit(solution)/shard_map/psum | solution.py:48
  332.6 663.5 %all-gather.6.cloned.1.call-start = ((), (), s32[]{:S(2)}) async-start(), calls=%async_computation.5 | async-start | bytes 8421376 | tf_op jit(solution)/shard_map/all_gather | solution.py:50
  581.3 575.1 %reduce-scatter.5.cloned.1.call-start = ((), (), s32[]{:S(2)}) async-start(), calls=%async_computation.6 | async-start | bytes 1081344 | tf_op jit(solution)/shard_map/reduce_scatter | solution.py:41
  581.4 414.7 %copy-start.4 = (f32[2,512,128]{2,1,0:T(8,128)S(1)}, f32[2,512,128]{2,1,0:T(8,128)}, u32[]{:S(2)}) copy-start(f32[2,512,128]{2,1,0:T(8,128)} %all-reduce.4.cloned.1.call-done) | copy-start | bytes 1572868
  581.4 419.6 %copy-start.3 = (f32[2,2048,128]{2,1,0:T(8,128)S(1)}, f32[2,2048,128]{2,1,0:T(8,128)}, u32[]{:S(2)}) copy-start(f32[2,2048,128]{2,1,0:T(8,128)} %all-gather.4.cloned.1.call-done) | copy-start | bytes 6291460
  996.1 4.9 copy-start.2
  1006.0 2.0 copy-start
  1016.1 389.0 %all-reduce.8.cloned.1.call-start = ((), (), s32[]{:S(2)}) async-start(), calls=%async_computation.7 | async-start | bytes 131072 | tf_op jit(solution)/shard_map/psum | solution.py:48
  1158.4 663.5 %all-gather.8.cloned.1.call-start = ((), (), s32[]{:S(2)}) async-start(), calls=%async_computation.8 | async-start | bytes 8421376 | tf_op jit(solution)/shard_map/all_gather | solution.py:50
  1821.9 4.9 copy-start.1
Sparse Core Ops, SparseCore 0:
  9.2 63.8 all-gather.3
  75.8 104.1 all-reduce.3
  188.1 142.4 reduce-scatter.6
  336.0 243.2 all-reduce.5
  581.5 414.6 all-gather.5
  1016.2 140.1 reduce-scatter.4
  1162.0 243.0 all-reduce.7
  1407.2 414.6 all-gather.7
where the time goes:
time: 1850 us
  waiting for transfers between devices  1770 us (96%)
  matrix products  43.8 us (2%)
    all_gather x2, waiting for transfers between devices, body(): w_all = lax.all_gather(w_own, ('row', 'col'), axis=0, tiled=True)  824 us
    psum x2, waiting for transfers between devices, body(): gram_matrix = lax.psum(mat_product(own_rows.T, ymatrix), ('row', 'col'))  493 us
    unnamed x9, waiting for transfers between devices  143 us
    reduce_scatter x1, waiting for transfers between devices, body(): lax.psum_scatter(partial_rows(jnp.int32(0), own_count * lax.axis_size('co...  140 us
    psum x1, waiting for transfers between devices, spread(): return lax.psum(block, axis)  105 us
    all_gather x1, waiting for transfers between devices, body(): v_rows = lax.all_gather(vectors, 'col', axis=1, tiled=True)  65.8 us
    dot_general x14, matrix products, mat_product(): jnp.dot(left, right, precision=highest, preferred_element_type=jnp.float32)  43.8 us
  transfers between devices with their start and end apart: 8, of which 8 were waited for; matrix products, arithmetic and copies ran while one was open for 0% of the time, Pallas kernels for 0%

commit v1 on v0

v1 whole, which is shorter than its diff:
```python
import jax
import jax.numpy as jnp
from jax import lax
from jax.experimental import pallas as pl
from jax.experimental.pallas import tpu as pltpu
from jax.sharding import PartitionSpec as P

MESH = pl.DeviceIdType.MESH
F32 = jnp.float32
BF16 = jnp.bfloat16
NN = ((1,), (0,))
TN = ((0,), (0,))


def split(value):
    high = value.astype(BF16)
    return high, (value - high.astype(F32)).astype(BF16)


def dot3(left, right, dims=NN):
    (lh, ll), (rh, rl) = left, right

    def one(a, b):
        return lax.dot_general(a, b, (dims, ((), ())), preferred_element_type=F32)

    return one(lh, rh) + (one(lh, rl) + one(ll, rh))


def dot_full(left, right):
    return jnp.dot(
        left, right, precision=lax.Precision.HIGHEST, preferred_element_type=F32
    )


def exchange_kernel(
    mat, vec, tf, vi_out, pi_out, xh_out, xl_out,
    a, vi, pi, vj, pj, part, ra, rb, ta, tb, fam, fap, fbp, fbm, total, l1,
    s1, s32, s2, s8, s3, sfull,
    send_sem, load_sem, zr, yr, cr, l2r, xr, rsr, l1r, s1r, s2r, s3r, s4r, s5r, s6r, out_sem,
):
    row, col = lax.axis_index("row"), lax.axis_index("col")
    x, zh = lax.div(row, 2), lax.rem(row, 2)
    y, zl, c = lax.div(col, 8), lax.rem(lax.div(col, 2), 4), lax.rem(col, 2)

    def mod4(v):
        return lax.rem(v + 8, 4)

    def dev(x_, zh_, y_, zl_, c_):
        return (x_ * 2 + zh_, (y_ * 4 + zl_) * 2 + c_)

    partner = dev(x, zh, y, zl, 1 - c)

    def at_x(k):
        return dev(mod4(x + k), zh, y, zl, c)

    def at_y(k):
        return dev(x, zh, mod4(y + k), zl, c)

    def at_zl(k):
        return dev(x, zh, y, mod4(zl + k), c)

    def at_z(k):
        z = lax.rem(zh * 4 + zl + k, 8)
        return dev(x, lax.div(z, 4), y, lax.rem(z, 4), c)

    def spread_to(h):
        return dev(zl, h, x, 2 * zh + lax.div(y, 2), lax.rem(y, 2))

    def owner(c_):
        return dev(y, lax.div(zl, 2), lax.rem(zl, 2) * 2 + c, x, c_)

    def is_me(d):
        return jnp.logical_and(d[0] == row, d[1] == col)

    def rows(ref, start, count):
        return ref.at[pl.ds(pl.multiple_of(start, 8), count)]

    def blk(ref, y_, zl_, c_):
        return rows(ref, ((y_ * 4 + zl_) * 2 + c_) * 64, 64)

    sent = []

    def send(src, dst, sem, device):
        copy = pltpu.make_async_remote_copy(
            src_ref=src, dst_ref=dst, send_sem=send_sem.at[len(sent)], recv_sem=sem,
            device_id=device, device_id_type=MESH,
        )
        copy.start()
        sent.append((copy, None))

    def send_or_keep(src, dst, sem, device):
        mine = is_me(device)
        copy = pltpu.make_async_remote_copy(
            src_ref=src, dst_ref=dst, send_sem=send_sem.at[len(sent)], recv_sem=sem,
            device_id=device, device_id_type=MESH,
        )
        keep = pltpu.make_async_copy(src, dst, sem)

        @pl.when(mine)
        def _():
            keep.start()

        @pl.when(jnp.logical_not(mine))
        def _():
            copy.start()

        sent.append((copy, jnp.logical_not(mine)))

    def arrived(dst, sem):
        pltpu.make_async_copy(dst, dst, sem).wait()

    load_a = pltpu.make_async_copy(mat, a, load_sem.at[0])
    own_v = blk(vi, y, zl, c)
    load_v = [
        pltpu.make_async_copy(
            vec.at[p],
            vi.at[pl.ds(pl.multiple_of(col * 64, 8), 64), pl.ds(128 * p, 128)],
            load_sem.at[1 + p],
        )
        for p in range(2)
    ]
    for copy in load_v:
        copy.start()
    load_a.start()

    barrier = pltpu.get_barrier_semaphore()
    peers = [partner] + [at_x(k) for k in (1, 2, 3)] + [at_y(k) for k in (1, 2, 3)]
    peers += [at_z(k) for k in range(1, 8)]
    for peer in peers:
        pl.semaphore_signal(barrier, inc=1, device_id=peer, device_id_type=MESH)
    for peer in (spread_to(0), spread_to(1), owner(0), owner(1)):

        @pl.when(jnp.logical_not(is_me(peer)))
        def _(peer=peer):
            pl.semaphore_signal(barrier, inc=1, device_id=peer, device_id_type=MESH)

    for copy in load_v:
        copy.wait()
    fixed = jnp.logical_or(is_me(spread_to(0)), is_me(spread_to(1)))
    pl.semaphore_wait(barrier, len(peers) + 4 - 2 * fixed.astype(jnp.int32))

    zk = [mod4(zl - k) for k in range(4)]
    yn = [y, mod4(y - 1), mod4(y + 1), mod4(y + 2)]

    def half(ref, y_, zl_, c_, h):
        return rows(ref, ((y_ * 4 + zl_) * 2 + c_) * 64 + 32 * h, 32)

    class Spread:
        def __init__(self, n, big, small):
            self.n, self.big, self.small = n, big, small

        def to_partner(self, n, k):
            b = blk(self.big, yn[n], zk[k], c)
            send(b, b, cr.at[self.n, n, k], partner)

        def to_y(self, k):
            b = blk(self.big, y, zk[k], c)
            send(b, b, yr.at[self.n, k, 0], at_y(1))
            send(b, b, yr.at[self.n, k, 1], at_y(3))

        def start(self):
            b = blk(self.big, y, zl, c)
            for k in (1, 2, 3):
                send(b, b, zr.at[self.n, k - 1], at_zl(k))
            self.to_y(0)
            self.to_partner(0, 0)
            d = rows(self.small, (2 * zl + c) * 64, 64)
            for h in range(2):
                send_or_keep(b, d, l2r.at[self.n, c], spread_to(h))

        def z_step(self):
            for k in (1, 2, 3):
                arrived(blk(self.big, y, zk[k], c), zr.at[self.n, k - 1])
                self.to_y(k)
                self.to_partner(0, k)

        def y_step(self, k):
            arrived(blk(self.big, yn[1], zk[k], c), yr.at[self.n, k, 0])
            h = half(self.big, yn[1], zk[k], c, 0)
            send(h, h, yr.at[self.n, k, 2], at_y(1))
            self.to_partner(1, k)
            arrived(blk(self.big, yn[2], zk[k], c), yr.at[self.n, k, 1])
            h = half(self.big, yn[2], zk[k], c, 1)
            send(h, h, yr.at[self.n, k, 3], at_y(3))
            self.to_partner(2, k)

        def y_last(self, k):
            for h in range(2):
                arrived(half(self.big, yn[3], zk[k], c, h), yr.at[self.n, k, 2 + h])
            self.to_partner(3, k)

        def from_partner(self, n):
            for k in range(4):
                arrived(blk(self.big, yn[n], zk[k], 1 - c), cr.at[self.n, n, k])

        def x_start(self):
            for h in range(2):
                arrived(rows(self.small, (2 * x + h) * 64, 64), l2r.at[self.n, h])
            b = rows(self.small, x * 128, 128)
            send(b, b, xr.at[self.n, 0], at_x(1))
            send(b, b, xr.at[self.n, 1], at_x(3))

        def x_step(self):
            m = mod4(x - 1)
            arrived(rows(self.small, m * 128, 128), xr.at[self.n, 0])
            h = rows(self.small, m * 128, 64)
            send(h, h, xr.at[self.n, 2], at_x(1))
            m = mod4(x + 1)
            arrived(rows(self.small, m * 128, 128), xr.at[self.n, 1])
            h = rows(self.small, m * 128 + 64, 64)
            send(h, h, xr.at[self.n, 3], at_x(3))

        def x_last(self):
            m = mod4(x + 2)
            for h in range(2):
                arrived(rows(self.small, m * 128 + 64 * h, 64), xr.at[self.n, 2 + h])

    sv = Spread(0, vi, vj)
    sv.start()
    sv.z_step()
    sv.x_start()
    for k in range(4):
        sv.y_step(k)
    sv.x_step()
    load_a.wait()

    def chunk(n):
        start = pl.multiple_of(yn[n] * 512, 512)
        vt = vi[pl.ds(start, 512), :].T
        return dot3(split(vt), split(a[pl.ds(start, 512), :]))

    sv.from_partner(0)
    pt = chunk(0)
    for k in range(4):
        sv.y_last(k)
    sv.from_partner(1)
    pt += chunk(1)
    sv.from_partner(2)
    pt += chunk(2)
    sv.x_last()
    sv.from_partner(3)
    pt += chunk(3)
    out_v = pltpu.make_async_copy(vi, vi_out, out_sem.at[0])
    out_v.start()

    pfull = pt.T
    for q in range(4):
        part[192 * q : 192 * q + 128, :] = pfull[128 * q : 128 * q + 128, :]
    s_part = dot3(split(vj[...].T), split(pfull))
    own = own_v[...]
    n_part = dot3(split(own[:, :128].T), split(own[:, 128:]))
    for q in range(2):
        part[192 * q + 128 : 192 * q + 192, :] = s_part[64 * q : 64 * q + 64, :]
    for q in range(2):
        low = slice(192 * (q + 2) + 128, 192 * (q + 2) + 192)
        part[low, :128] = n_part[64 * q : 64 * q + 64, :]
        part[low, 128:] = s_part[128 + 64 * q : 192 + 64 * q, 128:]

    def piece(k, h):
        return rows(part, mod4(x + k) * 192 + 96 * h, 96)

    send(piece(2, 0), ra, rsr.at[0], at_x(1))
    send(piece(2, 1), rb, rsr.at[1], at_x(3))
    send(piece(1, 1), fbm, rsr.at[2], at_x(1))
    send(piece(3, 0), fap, rsr.at[3], at_x(3))
    arrived(ra, rsr.at[0])
    ta[...] = ra[...] + piece(1, 0)[...]
    send(ta, fam, rsr.at[4], at_x(1))
    arrived(rb, rsr.at[1])
    tb[...] = rb[...] + piece(3, 1)[...]
    send(tb, fbp, rsr.at[5], at_x(3))
    arrived(fap, rsr.at[3])
    arrived(fbm, rsr.at[2])
    arrived(fam, rsr.at[4])
    total[0:96, :] = piece(0, 0)[...] + (fam[...] + fap[...])
    arrived(fbp, rsr.at[5])
    total[96:192, :] = piece(0, 1)[...] + (fbp[...] + fbm[...])

    for h in range(2):
        send_or_keep(total.at[pl.ds(64 * h, 64)], l1.at[zh], l1r.at[zh], owner(h))
    send(rows(total, 128 + 32 * (1 - c), 32), s1, s1r, partner)
    arrived(s1, s1r)
    s32[...] = rows(total, 128 + 32 * c, 32)[...] + s1[...]
    for k in (1, 2, 3):
        send(rows(s32, 8 * mod4(y + k), 8), s2.at[k - 1], s2r.at[k - 1], at_y(k))
    for h in range(2):
        arrived(l1.at[h], l1r.at[h])
    blk(pi, y, zl, c)[...] = l1[0] + l1[1]
    sp = Spread(1, pi, pj)
    sp.start()
    for k in range(3):
        arrived(s2.at[k], s2r.at[k])
    s8[...] = rows(s32, 8 * y, 8)[...] + s2[0] + (s2[1] + s2[2])
    for k in range(1, 8):
        send(s8, s3.at[k - 1], s3r.at[k - 1], at_z(k))
    sp.z_step()
    for k in range(7):
        arrived(s3.at[k], s3r.at[k])
    mine = s8[...] + s3[0] + (s3[1] + s3[2]) + ((s3[3] + s3[4]) + (s3[5] + s3[6]))

    def srow(x_, y_, c_):
        return rows(sfull, 64 * x_ + 32 * c_ + 8 * y_, 8)

    srow(x, y, c)[...] = mine
    for k in (1, 2, 3):
        send(srow(x, y, c), srow(x, y, c), s4r.at[k - 1], at_y(k))
    sp.x_start()
    sp.y_step(0)
    sp.y_step(1)
    for k in (1, 2, 3):
        arrived(srow(x, mod4(y - k), c), s4r.at[k - 1])
    s_own = rows(sfull, 64 * x + 32 * c, 32)
    for k in (1, 2, 3):
        send(s_own, s_own, s5r.at[k - 1], at_x(k))
    send(s_own, s_own, s6r.at[0], partner)
    sp.y_step(2)
    sp.y_step(3)
    sp.x_step()
    for k in (1, 2, 3):
        s_k = rows(sfull, 64 * mod4(x - k) + 32 * c, 32)
        arrived(s_k, s5r.at[k - 1])
        send(s_k, s_k, s6r.at[k], partner)
    for k in range(4):
        sp.y_last(k)
    for k in range(4):
        arrived(rows(sfull, 64 * mod4(x - k) + 32 * (1 - c), 32), s6r.at[k])

    upper = lax.broadcasted_iota(jnp.int32, (128, 128), 0) <= lax.broadcasted_iota(
        jnp.int32, (128, 128), 1
    )
    t1 = jnp.where(upper, tf[0], 0.0)
    t2 = jnp.where(upper, tf[1], 0.0)
    s11, s12 = sfull[0:128, 0:128], sfull[0:128, 128:256]
    n12, s22 = sfull[128:256, 0:128], sfull[128:256, 128:256]
    t1t, t2t = t1.T, t2.T
    b = dot_full(t1t, dot_full(s11, t1))
    e = dot_full(t1t, s12)
    h = dot_full(b.T, n12)
    nt2 = dot_full(n12, t2)
    f = dot_full(n12.T, e - 0.5 * h)
    k12 = dot_full(h - e, t2)
    m12 = -dot_full(t1, nt2)
    b2 = dot_full(t2t, dot_full(s22 - f - f.T, t2))
    zero = jnp.zeros((128, 128), F32)
    kk = jnp.concatenate(
        [
            jnp.concatenate([-0.5 * (b + b.T), k12], axis=1),
            jnp.concatenate([k12.T, -0.5 * (b2 + b2.T)], axis=1),
        ],
        axis=0,
    )
    mm = jnp.concatenate(
        [jnp.concatenate([t1, m12], axis=1), jnp.concatenate([zero, t2], axis=1)], axis=0
    )
    sp.x_last()
    m_s = split(mm)
    v_s = split(vj[...])
    xj = dot3(split(pj[...]), m_s) + dot3(v_s, split(kk))
    zj = dot3(v_s, split(mm.T))
    for n, value in enumerate((xj, zj)):
        high, low = split(value.T)
        xh_out[256 * n : 256 * n + 256, :] = high
        xl_out[256 * n : 256 * n + 256, :] = low

    for n in range(4):
        sp.from_partner(n)
    out_p = pltpu.make_async_copy(pi, pi_out, out_sem.at[1])
    out_p.start()
    for copy, when in sent:
        if when is None:
            copy.wait_send()
        else:

            @pl.when(when)
            def _(copy=copy):
                copy.wait_send()

    out_v.wait()
    out_p.wait()


def exchange(matrix, vectors, tfactor):
    def vmem(*shape):
        return pltpu.VMEM(shape, F32)

    def dma(*shape):
        return pltpu.SemaphoreType.DMA(shape)

    return pl.pallas_call(
        exchange_kernel,
        out_shape=(
            jax.ShapeDtypeStruct((2048, 256), F32),
            jax.ShapeDtypeStruct((2048, 256), F32),
            jax.ShapeDtypeStruct((512, 512), BF16),
            jax.ShapeDtypeStruct((512, 512), BF16),
        ),
        in_specs=[
            pl.BlockSpec(memory_space=pl.ANY),
            pl.BlockSpec(memory_space=pl.ANY),
            pl.BlockSpec(memory_space=pltpu.VMEM),
        ],
        out_specs=(
            pl.BlockSpec(memory_space=pl.ANY),
            pl.BlockSpec(memory_space=pl.ANY),
            pl.BlockSpec(memory_space=pltpu.VMEM),
            pl.BlockSpec(memory_space=pltpu.VMEM),
        ),
        scratch_shapes=[
            vmem(2048, 512), vmem(2048, 256), vmem(2048, 256), vmem(512, 256), vmem(512, 256),
            vmem(768, 256), vmem(96, 256), vmem(96, 256), vmem(96, 256), vmem(96, 256),
            vmem(96, 256), vmem(96, 256), vmem(96, 256), vmem(96, 256), vmem(192, 256),
            vmem(2, 64, 256), vmem(32, 256), vmem(32, 256), vmem(3, 8, 256), vmem(8, 256),
            vmem(7, 8, 256), vmem(256, 256),
            dma(160), dma(3), dma(2, 3), dma(2, 4, 4), dma(2, 4, 4), dma(2, 2), dma(2, 4),
            dma(6), dma(2), dma(), dma(3), dma(7), dma(3), dma(3), dma(4), dma(2),
        ],
        compiler_params=pltpu.CompilerParams(
            collective_id=0, has_side_effects=True, vmem_limit_bytes=48 << 20
        ),
    )(matrix, vectors, tfactor)


def update_kernel(mat, vi, pi, xh, xl, out):
    left = split(jnp.concatenate([vi[...], pi[...]], axis=1))
    out[...] = mat[...] - dot3(left, (xh[...], xl[...]))


def update(matrix, vi, pi, xh, xl):
    rows_here, cols_here = matrix.shape
    step = 512
    return pl.pallas_call(
        update_kernel,
        grid=(rows_here // step,),
        out_shape=jax.ShapeDtypeStruct(matrix.shape, F32),
        in_specs=[
            pl.BlockSpec((step, cols_here), lambda i: (i, 0)),
            pl.BlockSpec((step, 256), lambda i: (i, 0)),
            pl.BlockSpec((step, 256), lambda i: (i, 0)),
            pl.BlockSpec((512, 512), lambda i: (0, 0)),
            pl.BlockSpec((512, 512), lambda i: (0, 0)),
        ],
        out_specs=pl.BlockSpec((step, cols_here), lambda i: (i, 0)),
        compiler_params=pltpu.CompilerParams(vmem_limit_bytes=32 << 20),
    )(matrix, vi, pi, xh, xl)


def body(matrix, vectors, tfactor):
    return update(matrix, *exchange(matrix, vectors, tfactor))


def solution(mesh):
    return jax.shard_map(
        body,
        mesh=mesh,
        in_specs=(P("row", "col"), P(None, ("row", "col"), None), P()),
        out_specs=P("row", "col"),
        check_vma=False,
    )
```

time: 1850 us -> 97.4 us (0.05)
  waiting for transfers between devices: 1770 us -> 0 us
  Pallas kernels: 0 us -> 95.2 us
  matrix products: 43.8 us -> 0 us
    all_gather x3 -> x0, waiting for transfers between devices: 890 us -> none  [the longest x2 824 us: body(): w_all = lax.all_gather(w_own, ('row', 'col'), axis=0, tiled=True)]
    psum x3 -> x0, waiting for transfers between devices: 598 us -> none  [the longest x2 493 us: body(): gram_matrix = lax.psum(mat_product(own_rows.T, ymatrix), ('row', 'col'))]
    unnamed x9 -> x0, waiting for transfers between devices: 143 us -> none
    reduce_scatter x1 -> x0, waiting for transfers between devices: 140 us -> none  [body(): lax.psum_scatter(partial_rows(jnp.int32(0), own_count * lax.axis_size('co...]
    pallas_call x0 -> x2, Pallas kernels: none -> 95.2 us  [the longest x1 90.2 us: exchange(): pl.pallas_call(exchange_kernel, out_shape=(jax.ShapeDtypeStruct((2048, 25...]
    dot_general x14 -> x0, matrix products: 43.8 us -> none  [mat_product(): jnp.dot(left, right, precision=highest, preferred_element_type=jnp.float32)]
  transfers between devices with their start and end apart: 8 -> 0, of which waited for: 8 -> 0; matrix products, arithmetic and copies ran while one was open for 0% -> 0% of each run, Pallas kernels for 0% -> 0%
where the time goes in v1:
time: 97.4 us; the launch traced here: 97.3 us
  Pallas kernels  95.2 us (98%)
  local copies, waits for them, and re-layouts  2.16 us (2%)
    pallas_call x1, Pallas kernels, exchange(): pl.pallas_call(exchange_kernel, out_shape=(jax.ShapeDtypeStruct((2048, 25...  90.2 us
    pallas_call x1, Pallas kernels, update(): pl.pallas_call(update_kernel, grid=(rows_here // step,), out_shape=jax.Sh...  4.94 us
    unnamed x6, local copies, waits for them, and re-layouts  2.16 us

profile of v1, /device:TPU:1, one launch (start us, length us, event | category | flops | bytes accessed | tf_op | source)
XLA Modules:
  0.0 97.3 jit_solution(16036978799850664430)
XLA Ops:
  0.0 0.0 copy-start
  0.0 0.0 copy-start.1
  0.0 1.1 %copy-done.1 = f32[2,128,128]{2,1,0:T(8,128)S(1)} copy-done((f32[2,128,128]{2,1,0:T(8,128)S(1)}, f32[2,128,128]{2,1,0:T(8,128)}, u32[]{:S(2)}) %copy-start.1) | copy-done | bytes 131096
  1.1 0.0 copy-start.2
  1.1 1.1 %copy-done.2 = f32[2,64,128]{2,1,0:T(8,128)S(1)} copy-done((f32[2,64,128]{2,1,0:T(8,128)S(1)}, f32[2,64,128]{2,1,0:T(8,128)}, u32[]{:S(2)}) %copy-start.2) | copy-done | bytes 65560
  2.2 90.2 %shard_map.37 = (f32[2048,256]{1,0:T(8,128)S(1)}, f32[2048,256]{1,0:T(8,128)S(1)}, bf16[512,512]{1,0:T(8,128)(2,1)S(1)}, bf16[512,512]{1,0:T(8,128)(2,1)S(1)}) custom-call(f32[2048,512]{1,0:T(8,128)} %mat.3, f32[2,64,128]{2,1,0:T(8,128)S(1)} %copy-done.2, f32[2,128,128]{2,1,0:T(8,128)S(1)} %copy-done.1), custom_call_target="tpu_custom_call" | custom-call | tf_op jit(solution)/shard_map/pallas_call | solution.py:389
  92.4 0.0 copy-done
  92.4 4.9 %shard_map.38 = f32[2048,512]{1,0:T(8,128)} custom-call(f32[2048,512]{1,0:T(8,128)S(1)} %copy-done, f32[2048,256]{1,0:T(8,128)S(1)} %get-tuple-element.9.vi, f32[2048,256]{1,0:T(8,128)S(1)} %get-tuple-element.10.pi, bf16[512,512]{1,0:T(8,128)(2,1)S(1)} %get-tuple-element.11.xh, bf16[512,512]{1,0:T(8,128)(2,1)S(1)} %get-tuple-element.12.xl), custom_call_target="tpu_custom_call" | custom-call | tf_op jit(solution)/shard_map/pallas_call | solution.py:431
Async XLA Ops:
  0.0 92.4 %copy-start = (f32[2048,512]{1,0:T(8,128)S(1)}, f32[2048,512]{1,0:T(8,128)}, u32[]{:S(2)}) copy-start(f32[2048,512]{1,0:T(8,128)} %mat.3) | copy-start | bytes 12582916
  0.0 1.1 %copy-start.1 = (f32[2,128,128]{2,1,0:T(8,128)S(1)}, f32[2,128,128]{2,1,0:T(8,128)}, u32[]{:S(2)}) copy-start(f32[2,128,128]{2,1,0:T(8,128)} %tf.1) | copy-start | bytes 393220
  1.1 1.1 %copy-start.2 = (f32[2,64,128]{2,1,0:T(8,128)S(1)}, f32[2,64,128]{2,1,0:T(8,128)}, u32[]{:S(2)}) copy-start(f32[2,64,128]{2,1,0:T(8,128)} %vec.1) | copy-start | bytes 196612

commit v2 on v1

v2 whole, which is shorter than its diff:
```python
import jax
import jax.numpy as jnp
from jax import lax
from jax.experimental import pallas as pl
from jax.experimental.pallas import tpu as pltpu
from jax.sharding import PartitionSpec as P

MESH = pl.DeviceIdType.MESH
F32 = jnp.float32
BF16 = jnp.bfloat16
NN = ((1,), (0,))
TN = ((0,), (0,))


def split(value):
    high = value.astype(BF16)
    return high, (value - high.astype(F32)).astype(BF16)


def dot3(left, right, dims=NN):
    (lh, ll), (rh, rl) = left, right

    def one(a, b):
        return lax.dot_general(a, b, (dims, ((), ())), preferred_element_type=F32)

    return one(lh, rh) + (one(lh, rl) + one(ll, rh))


def dot_full(left, right):
    return jnp.dot(
        left, right, precision=lax.Precision.HIGHEST, preferred_element_type=F32
    )


def exchange_kernel(
    mat, vec, tf, a2, pi, zh_out, zl_out,
    a, vi, vj, pj, part, ra, rb, ta, tb, fam, fap, fbp, fbm, total, l1, hx,
    sp_, s1, s128, sx, s32, sy, s8, sz, sfull, tfv,
    send_sem, load_sem, zr, yr, cr, l2r, xr, rsr, l1r, hr, s1r, sxr, syr, szr, s4r, s5r, s6r,
):
    row, col = lax.axis_index("row"), lax.axis_index("col")
    x, zh = lax.div(row, 2), lax.rem(row, 2)
    y, zl, c = lax.div(col, 8), lax.rem(lax.div(col, 2), 4), lax.rem(col, 2)

    def mod4(v):
        return lax.rem(v + 8, 4)

    def dev(x_, zh_, y_, zl_, c_):
        return (x_ * 2 + zh_, (y_ * 4 + zl_) * 2 + c_)

    partner = dev(x, zh, y, zl, 1 - c)

    def at_x(k):
        return dev(mod4(x + k), zh, y, zl, c)

    def at_y(k):
        return dev(x, zh, mod4(y + k), zl, c)

    zk = [zl, zl + 1 - 2 * lax.rem(zl, 2), mod4(zl + 2), 3 - zl]
    yn = [y, mod4(y - 1), mod4(y + 1), mod4(y + 2)]

    def at_zl(k):
        return dev(x, zh, y, zk[k], c)

    def at_z(k):
        z = lax.rem(zh * 4 + zl + k, 8)
        return dev(x, lax.div(z, 4), y, lax.rem(z, 4), c)

    def spread_to(h):
        return dev(zl, h, x, 2 * zh + lax.div(y, 2), lax.rem(y, 2))

    def spread_from(h):
        return dev(y, lax.div(zl, 2), lax.rem(zl, 2) * 2 + c, x, h)

    def owner(h):
        return dev(y, lax.div(zl, 2), x, lax.rem(zl, 2) * 2 + c, h)

    def owned_from(h):
        return dev(y, h, x, 2 * zh + lax.div(zl, 2), lax.rem(zl, 2))

    def is_me(d):
        return jnp.logical_and(d[0] == row, d[1] == col)

    def rows(ref, start, count):
        return ref.at[pl.ds(pl.multiple_of(start, 8), count)]

    sent = []

    def send(src, dst, sem, device):
        copy = pltpu.make_async_remote_copy(
            src_ref=src, dst_ref=dst, send_sem=send_sem.at[len(sent)], recv_sem=sem,
            device_id=device, device_id_type=MESH,
        )
        copy.start()
        sent.append((copy, None))

    def send_or_keep(src, dst, sem, device):
        mine = is_me(device)
        copy = pltpu.make_async_remote_copy(
            src_ref=src, dst_ref=dst, send_sem=send_sem.at[len(sent)], recv_sem=sem,
            device_id=device, device_id_type=MESH,
        )
        keep = pltpu.make_async_copy(src, dst, sem)

        @pl.when(mine)
        def _():
            keep.start()

        @pl.when(jnp.logical_not(mine))
        def _():
            copy.start()

        sent.append((copy, jnp.logical_not(mine)))

    def finish():
        for copy, when in sent:
            if when is None:
                copy.wait_send()
            else:

                @pl.when(when)
                def _(copy=copy):
                    copy.wait_send()

    def arrived(dst, sem):
        pltpu.make_async_copy(dst, dst, sem).wait()

    load_a = pltpu.make_async_copy(mat, a, load_sem.at[0])
    load_t = pltpu.make_async_copy(tf, tfv, load_sem.at[3])
    load_v = [
        pltpu.make_async_copy(
            vec.at[p],
            vi.at[pl.ds(pl.multiple_of(col * 64, 8), 64), pl.ds(128 * p, 128)],
            load_sem.at[1 + p],
        )
        for p in range(2)
    ]
    for copy in load_v:
        copy.start()
    load_a.start()
    load_t.start()

    barrier = pltpu.get_barrier_semaphore()
    peers = [partner] + [at_x(k) for k in (1, 2, 3)] + [at_y(k) for k in (1, 2, 3)]
    peers += [at_z(k) for k in range(1, 8)]
    for peer in peers:
        pl.semaphore_signal(barrier, inc=1, device_id=peer, device_id_type=MESH)
    others = [f(h) for f in (spread_to, spread_from, owner, owned_from) for h in range(2)]
    for peer in others:

        @pl.when(jnp.logical_not(is_me(peer)))
        def _(peer=peer):
            pl.semaphore_signal(barrier, inc=1, device_id=peer, device_id_type=MESH)

    for copy in load_v:
        copy.wait()
    count = len(peers) + len(others)
    for peer in others:
        count = count - is_me(peer).astype(jnp.int32)
    pl.semaphore_wait(barrier, count)

    class Gather:
        def __init__(self, n, big, place):
            self.n, self.big, self.place = n, big, place

        def blk(self, y_, zl_, c_):
            return rows(self.big, self.place(y_, zl_, c_) * 64, 64)

        def half(self, y_, zl_, c_, h):
            return rows(self.big, self.place(y_, zl_, c_) * 64 + 32 * h, 32)

        def to_partner(self, n, k):
            b = self.blk(yn[n], zk[k], c)
            send(b, b, cr.at[self.n, n, k], partner)

        def to_y(self, k):
            b = self.blk(y, zk[k], c)
            send(b, b, yr.at[self.n, k, 0], at_y(1))
            send(b, b, yr.at[self.n, k, 1], at_y(3))

        def start(self):
            b = self.blk(y, zl, c)
            for k in (1, 2, 3):
                send(b, b, zr.at[self.n, k - 1], at_zl(k))
            self.to_y(0)
            self.to_partner(0, 0)

        def z_step(self, k):
            arrived(self.blk(y, zk[k], c), zr.at[self.n, k - 1])
            self.to_y(k)
            self.to_partner(0, k)

        def y_step(self, k):
            arrived(self.blk(yn[1], zk[k], c), yr.at[self.n, k, 0])
            h = self.half(yn[1], zk[k], c, 0)
            send(h, h, yr.at[self.n, k, 2], at_y(1))
            self.to_partner(1, k)
            arrived(self.blk(yn[2], zk[k], c), yr.at[self.n, k, 1])
            h = self.half(yn[2], zk[k], c, 1)
            send(h, h, yr.at[self.n, k, 3], at_y(3))
            self.to_partner(2, k)

        def y_last(self, k):
            for h in range(2):
                arrived(self.half(yn[3], zk[k], c, h), yr.at[self.n, k, 2 + h])
            self.to_partner(3, k)

        def from_partner(self, n):
            for k in range(4):
                arrived(self.blk(yn[n], zk[k], 1 - c), cr.at[self.n, n, k])

    class Ring:
        def __init__(self, n, small):
            self.n, self.small = n, small

        def start(self):
            b = rows(self.small, x * 128, 128)
            send(b, b, xr.at[self.n, 0], at_x(1))
            send(b, b, xr.at[self.n, 1], at_x(3))

        def step(self):
            m = mod4(x - 1)
            arrived(rows(self.small, m * 128, 128), xr.at[self.n, 0])
            h = rows(self.small, m * 128, 64)
            send(h, h, xr.at[self.n, 2], at_x(1))
            m = mod4(x + 1)
            arrived(rows(self.small, m * 128, 128), xr.at[self.n, 1])
            h = rows(self.small, m * 128 + 64, 64)
            send(h, h, xr.at[self.n, 3], at_x(3))

        def last(self):
            m = mod4(x + 2)
            for h in range(2):
                arrived(rows(self.small, m * 128 + 64 * h, 64), xr.at[self.n, 2 + h])

    gv = Gather(0, vi, lambda y_, zl_, c_: (y_ * 4 + zl_) * 2 + c_)
    rv = Ring(0, vj)
    gv.start()
    for h in range(2):
        send_or_keep(
            gv.blk(y, zl, c), rows(vj, (2 * zl + c) * 64, 64), l2r.at[c], spread_to(h)
        )
    for k in (1, 2, 3):
        gv.z_step(k)
    for k in range(3):
        gv.y_step(k)
    for h in range(2):
        arrived(rows(vj, (2 * x + h) * 64, 64), l2r.at[h])
    rv.start()
    gv.y_step(3)
    load_a.wait()
    load_t.wait()

    def chunk(n):
        start = pl.multiple_of(yn[n] * 512, 512)
        vt = vi[pl.ds(start, 512), :].T
        return dot3(split(vt), split(a[pl.ds(start, 512), :]))

    gv.from_partner(0)
    pt = chunk(0)
    rv.step()
    for k in range(4):
        gv.y_last(k)
    gv.from_partner(1)
    pt += chunk(1)
    gv.from_partner(2)
    pt += chunk(2)
    gv.from_partner(3)
    pt += chunk(3)
    part[...] = pt.T

    def piece(k, h):
        return rows(part, mod4(x + k) * 128 + 64 * h, 64)

    send(piece(2, 0), ra, rsr.at[0], at_x(1))
    send(piece(2, 1), rb, rsr.at[1], at_x(3))
    send(piece(1, 1), fbm, rsr.at[2], at_x(1))
    send(piece(3, 0), fap, rsr.at[3], at_x(3))

    rv.last()
    sp_[...] = dot3(split(vj[...].T), split(part[...]))
    own = gv.blk(y, zl, c)[...]
    sp_[128:256, 0:128] = dot3(split(own[:, :128].T), split(own[:, 128:]))
    send(rows(sp_, 128 * (1 - c), 128), s1, s1r, partner)
    arrived(s1, s1r)
    s128[...] = rows(sp_, 128 * c, 128)[...] + s1[...]
    for k in (1, 2, 3):
        send(rows(s128, 32 * mod4(x + k), 32), sx.at[k - 1], sxr.at[k - 1], at_x(k))

    arrived(ra, rsr.at[0])
    ta[...] = ra[...] + piece(1, 0)[...]
    send(ta, fam, rsr.at[4], at_x(1))
    arrived(rb, rsr.at[1])
    tb[...] = rb[...] + piece(3, 1)[...]
    send(tb, fbp, rsr.at[5], at_x(3))
    for k in range(3):
        arrived(sx.at[k], sxr.at[k])
    s32[...] = rows(s128, 32 * x, 32)[...] + sx[0] + (sx[1] + sx[2])
    for k in (1, 2, 3):
        send(rows(s32, 8 * mod4(y + k), 8), sy.at[k - 1], syr.at[k - 1], at_y(k))
    arrived(fap, rsr.at[3])
    arrived(fbm, rsr.at[2])
    arrived(fam, rsr.at[4])
    total[0:64, :] = piece(0, 0)[...] + (fam[...] + fap[...])
    send_or_keep(total.at[pl.ds(0, 64)], l1.at[zh], l1r.at[zh], owner(0))
    arrived(fbp, rsr.at[5])
    total[64:128, :] = piece(0, 1)[...] + (fbp[...] + fbm[...])
    send_or_keep(total.at[pl.ds(64, 64)], l1.at[zh], l1r.at[zh], owner(1))
    send(total, hx, hr, at_z(4))

    for k in range(3):
        arrived(sy.at[k], syr.at[k])
    s8[...] = rows(s32, 8 * y, 8)[...] + sy[0] + (sy[1] + sy[2])
    for k in range(1, 8):
        send(s8, sz.at[k - 1], szr.at[k - 1], at_z(k))
    arrived(hx, hr)
    rp = Ring(1, pj)
    rows(pj, x * 128, 128)[...] = total[...] + hx[...]
    rp.start()
    for h in range(2):
        arrived(l1.at[h], l1r.at[h])
    gp = Gather(1, pi, lambda y_, zl_, c_: (zl_ * 4 + y_) * 2 + c_)
    gp.blk(y, zl, c)[...] = l1[0] + l1[1]
    gp.start()

    def srow(x_, y_, c_):
        return rows(sfull, 128 * c_ + 32 * x_ + 8 * y_, 8)

    for k in range(7):
        arrived(sz.at[k], szr.at[k])
    srow(x, y, c)[...] = s8[...] + sz[0] + (sz[1] + sz[2]) + ((sz[3] + sz[4]) + (sz[5] + sz[6]))
    for k in (1, 2, 3):
        send(srow(x, y, c), srow(x, y, c), s4r.at[k - 1], at_y(k))
    gp.z_step(1)
    rp.step()
    for k in (1, 2, 3):
        arrived(srow(x, mod4(y - k), c), s4r.at[k - 1])
    s_own = rows(sfull, 128 * c + 32 * x, 32)
    for k in (1, 2, 3):
        send(s_own, s_own, s5r.at[k - 1], at_x(k))
    send(s_own, s_own, s6r.at[0], partner)
    gp.z_step(2)
    gp.z_step(3)
    gp.y_step(0)
    for k in (1, 2, 3):
        s_k = rows(sfull, 128 * c + 32 * mod4(x - k), 32)
        arrived(s_k, s5r.at[k - 1])
        send(s_k, s_k, s6r.at[k], partner)
    rp.last()
    gp.y_step(1)
    for k in range(4):
        arrived(rows(sfull, 128 * (1 - c) + 32 * mod4(x - k), 32), s6r.at[k])

    upper = lax.broadcasted_iota(jnp.int32, (128, 128), 0) <= lax.broadcasted_iota(
        jnp.int32, (128, 128), 1
    )
    t1 = jnp.where(upper, tfv[0], 0.0)
    t2 = jnp.where(upper, tfv[1], 0.0)
    s11, s12 = sfull[0:128, 0:128], sfull[0:128, 128:256]
    n12, s22 = sfull[128:256, 0:128], sfull[128:256, 128:256]
    t1t, t2t = t1.T, t2.T
    b = dot_full(t1t, dot_full(s11, t1))
    e = dot_full(t1t, s12)
    h = dot_full(b.T, n12)
    gp.y_step(2)
    nt2 = dot_full(n12, t2)
    f = dot_full(n12.T, e - 0.5 * h)
    k12 = dot_full(h - e, t2)
    m12 = -dot_full(t1, nt2)
    b2 = dot_full(t2t, dot_full(s22 - f - f.T, t2))
    gp.y_step(3)
    zero = jnp.zeros((128, 128), F32)
    kk = jnp.concatenate(
        [
            jnp.concatenate([-0.5 * (b + b.T), k12], axis=1),
            jnp.concatenate([k12.T, -0.5 * (b2 + b2.T)], axis=1),
        ],
        axis=0,
    )
    mm = jnp.concatenate(
        [jnp.concatenate([t1, m12], axis=1), jnp.concatenate([zero, t2], axis=1)], axis=0
    )
    v_s = split(vj[...])
    xj = dot3(split(pj[...]), split(mm)) + dot3(v_s, split(kk))
    zj = dot3(v_s, split(mm.T))
    zh_out[...], zl_out[...] = split(zj.T)
    x_s = split(xj.T)
    gp.y_last(0)
    gp.y_last(1)
    for n in range(4):
        r = slice(512 * n, 512 * n + 512)
        a2[r, :] = a[r, :] - dot3(split(vi[r, :]), x_s)
        if n == 0:
            gp.y_last(2)
            gp.y_last(3)
    for n in range(4):
        gp.from_partner(n)
    finish()


def exchange(matrix, vectors, tfactor):
    def vmem(*shape):
        return pltpu.VMEM(shape, F32)

    def dma(*shape):
        return pltpu.SemaphoreType.DMA(shape)

    return pl.pallas_call(
        exchange_kernel,
        out_shape=(
            jax.ShapeDtypeStruct((2048, 512), F32),
            jax.ShapeDtypeStruct((2048, 256), F32),
            jax.ShapeDtypeStruct((256, 512), BF16),
            jax.ShapeDtypeStruct((256, 512), BF16),
        ),
        in_specs=[pl.BlockSpec(memory_space=pltpu.HBM)] * 3,
        out_specs=(pl.BlockSpec(memory_space=pltpu.VMEM),) * 4,
        scratch_shapes=[
            vmem(2048, 512), vmem(2048, 256), vmem(512, 256), vmem(512, 256), vmem(512, 256),
            vmem(64, 256), vmem(64, 256), vmem(64, 256), vmem(64, 256),
            vmem(64, 256), vmem(64, 256), vmem(64, 256), vmem(64, 256), vmem(128, 256),
            vmem(2, 64, 256), vmem(128, 256),
            vmem(256, 256), vmem(128, 256), vmem(128, 256), vmem(3, 32, 256), vmem(32, 256),
            vmem(3, 8, 256), vmem(8, 256), vmem(7, 8, 256), vmem(256, 256), vmem(2, 128, 128),
            dma(160), dma(4), dma(2, 3), dma(2, 4, 4), dma(2, 4, 4), dma(2), dma(2, 4),
            dma(6), dma(2), dma(), dma(), dma(3), dma(3), dma(7), dma(3), dma(3), dma(4),
        ],
        compiler_params=pltpu.CompilerParams(
            collective_id=0, has_side_effects=True, vmem_limit_bytes=36 << 20
        ),
    )(*(pltpu.with_memory_space_constraint(v, pltpu.HBM) for v in (matrix, vectors, tfactor)))


def update_kernel(mat, pi, zh, zl, out):
    out[...] = mat[...] - dot3(split(pi[...]), (zh[...], zl[...]))


def update(matrix, pi, zh, zl):
    rows_here, cols_here = matrix.shape
    step = 512
    return pl.pallas_call(
        update_kernel,
        grid=(rows_here // step,),
        out_shape=jax.ShapeDtypeStruct(matrix.shape, F32),
        in_specs=[
            pl.BlockSpec((step, cols_here), lambda i: (i, 0)),
            pl.BlockSpec((step, 256), lambda i: (i, 0)),
            pl.BlockSpec((256, 512), lambda i: (0, 0)),
            pl.BlockSpec((256, 512), lambda i: (0, 0)),
        ],
        out_specs=pl.BlockSpec((step, cols_here), lambda i: (i, 0)),
        compiler_params=pltpu.CompilerParams(vmem_limit_bytes=20 << 20),
    )(matrix, pi, zh, zl)


def body(matrix, vectors, tfactor):
    return update(*exchange(matrix, vectors, tfactor))


def solution(mesh):
    return jax.shard_map(
        body,
        mesh=mesh,
        in_specs=(P("row", "col"), P(None, ("row", "col"), None), P()),
        out_specs=P("row", "col"),
        check_vma=False,
    )
```

time: 97.4 us -> 81.6 us (0.84)
  Pallas kernels: 95.2 us -> 81.5 us
  local copies, waits for them, and re-layouts: 2.16 us -> 0 us
    pallas_call x1, Pallas kernels: 90.2 us -> 77.7 us  [exchange(): pl.pallas_call(exchange_kernel, out_shape=(jax.ShapeDtypeStruct((2048, 51...]
    unnamed x6 -> x0, local copies, waits for them, and re-layouts: 2.16 us -> none
    pallas_call x1, Pallas kernels: 4.94 us -> 3.75 us  [update(): pl.pallas_call(update_kernel, grid=(rows_here // step,), out_shape=jax.Sh...]
where the time goes in v2:
time: 81.6 us; the launch traced here: 81.5 us
  Pallas kernels  81.5 us (100%)
    pallas_call x1, Pallas kernels, exchange(): pl.pallas_call(exchange_kernel, out_shape=(jax.ShapeDtypeStruct((2048, 51...  77.7 us
    pallas_call x1, Pallas kernels, update(): pl.pallas_call(update_kernel, grid=(rows_here // step,), out_shape=jax.Sh...  3.75 us

profile of v2, /device:TPU:1, one launch (start us, length us, event | category | flops | bytes accessed | tf_op | source)
XLA Modules:
  0.0 81.5 jit_solution(5097837684637440513)
XLA Ops:
  0.0 77.7 %shard_map.37 = (f32[2048,512]{1,0:T(8,128)S(1)}, f32[2048,256]{1,0:T(8,128)S(1)}, bf16[256,512]{1,0:T(8,128)(2,1)S(1)}, bf16[256,512]{1,0:T(8,128)(2,1)S(1)}) custom-call(f32[2048,512]{1,0:T(8,128)} %mat.1, f32[2,64,128]{2,1,0:T(8,128)} %vec.1, f32[2,128,128]{2,1,0:T(8,128)} %tf.1), custom_call_target="tpu_custom_call" | custom-call | tf_op jit(solution)/shard_map/pallas_call | solution.py:408
  77.8 3.8 %shard_map.38 = f32[2048,512]{1,0:T(8,128)} custom-call(f32[2048,512]{1,0:T(8,128)S(1)} %get-tuple-element.9.mat, f32[2048,256]{1,0:T(8,128)S(1)} %get-tuple-element.10.pi, bf16[256,512]{1,0:T(8,128)(2,1)S(1)} %get-tuple-element.11.zh, bf16[256,512]{1,0:T(8,128)(2,1)S(1)} %get-tuple-element.12.zl), custom_call_target="tpu_custom_call" | custom-call | tf_op jit(solution)/shard_map/pallas_call | solution.py:441

commit v3 on v2

--- a/solution.py
+++ b/solution.py
@@ -34,9 +34,10 @@
 
 def exchange_kernel(
     mat, vec, tf, a2, pi, zh_out, zl_out,
-    a, vi, vj, pj, part, ra, rb, ta, tb, fam, fap, fbp, fbm, total, l1, hx,
+    a, vi, vj, pj, part, xb, total, hx, q, qr, yb, qz, zb,
     sp_, s1, s128, sx, s32, sy, s8, sz, sfull, tfv,
-    send_sem, load_sem, zr, yr, cr, l2r, xr, rsr, l1r, hr, s1r, sxr, syr, szr, s4r, s5r, s6r,
+    send_sem, load_sem, zr, yr, cr, l2r, xr, rsr, hr, qcr, yqr, zqr,
+    s1r, sxr, syr, szr, s4r, s5r, s6r,
 ):
     row, col = lax.axis_index("row"), lax.axis_index("col")
     x, zh = lax.div(row, 2), lax.rem(row, 2)
@@ -71,12 +72,6 @@
 
     def spread_from(h):
         return dev(y, lax.div(zl, 2), lax.rem(zl, 2) * 2 + c, x, h)
-
-    def owner(h):
-        return dev(y, lax.div(zl, 2), x, lax.rem(zl, 2) * 2 + c, h)
-
-    def owned_from(h):
-        return dev(y, h, x, 2 * zh + lax.div(zl, 2), lax.rem(zl, 2))
 
     def is_me(d):
         return jnp.logical_and(d[0] == row, d[1] == col)
@@ -145,7 +140,7 @@
     peers += [at_z(k) for k in range(1, 8)]
     for peer in peers:
         pl.semaphore_signal(barrier, inc=1, device_id=peer, device_id_type=MESH)
-    others = [f(h) for f in (spread_to, spread_from, owner, owned_from) for h in range(2)]
+    others = [f(h) for f in (spread_to, spread_from) for h in range(2)]
     for peer in others:
 
         @pl.when(jnp.logical_not(is_me(peer)))
@@ -233,23 +228,77 @@
             for h in range(2):
                 arrived(rows(self.small, m * 128 + 64 * h, 64), xr.at[self.n, 2 + h])
 
-    gv = Gather(0, vi, lambda y_, zl_, c_: (y_ * 4 + zl_) * 2 + c_)
+    class Sum:
+        def __init__(self, at, piece, buf, sem):
+            self.at, self.piece, self.buf, self.sem = at, piece, buf, sem
+
+        def first(self):
+            send(self.piece(2, 0), self.buf(0), self.sem(0), self.at(1))
+            send(self.piece(2, 1), self.buf(1), self.sem(1), self.at(3))
+            send(self.piece(1, 1), self.buf(2), self.sem(2), self.at(1))
+            send(self.piece(3, 0), self.buf(3), self.sem(3), self.at(3))
+
+        def second(self):
+            for h, k, to in ((0, 1, 1), (1, 3, 3)):
+                arrived(self.buf(h), self.sem(h))
+                self.buf(6 + h)[...] = self.buf(h)[...] + self.piece(k, h)[...]
+                send(self.buf(6 + h), self.buf(4 + h), self.sem(4 + h), self.at(to))
+
+        def last(self, out):
+            for h in range(2):
+                arrived(self.buf(3 - h), self.sem(3 - h))
+                arrived(self.buf(4 + h), self.sem(4 + h))
+                out(h)[...] = self.piece(0, h)[...] + (self.buf(4 + h)[...] + self.buf(3 - h)[...])
+
+    def place(y_, zl_, c_):
+        return (y_ * 4 + zl_) * 2 + c_
+
+    gv = Gather(0, vi, place)
     rv = Ring(0, vj)
-    gv.start()
     for h in range(2):
         send_or_keep(
             gv.blk(y, zl, c), rows(vj, (2 * zl + c) * 64, 64), l2r.at[c], spread_to(h)
         )
+    gv.start()
     for k in (1, 2, 3):
         gv.z_step(k)
-    for k in range(3):
-        gv.y_step(k)
     for h in range(2):
         arrived(rows(vj, (2 * x + h) * 64, 64), l2r.at[h])
     rv.start()
-    gv.y_step(3)
+    for k in range(4):
+        gv.y_step(k)
+    rv.step()
+    for k in range(4):
+        gv.y_last(k)
     load_a.wait()
     load_t.wait()
+    rv.last()
+
+    v_s = split(vj[...])
+    gq = Gather(2, q, place)
+    gr = Gather(2, qr, place)
+    for n in (3, 1, 2, 0):
+        span = pl.ds(pl.multiple_of(yn[n] * 512, 512), 512)
+        q[span, :] = dot3(split(a[span, :]), v_s)
+        for k in (3, 2, 1, 0):
+            send(
+                gq.blk(yn[n], zk[k], 1 - c), gr.blk(yn[n], zk[k], 1 - c), qcr.at[n, k], partner
+            )
+    ysum = []
+    for k in (3, 2, 1, 0):
+        for n in (3, 1, 2, 0):
+            arrived(gr.blk(yn[n], zk[k], c), qcr.at[n, k])
+            b = gq.blk(yn[n], zk[k], c)
+            b[...] = b[...] + gr.blk(yn[n], zk[k], c)[...]
+        ysum.append(
+            Sum(
+                at_y,
+                lambda m, h, k=k: gq.half(mod4(y + m), zk[k], c, h),
+                lambda m, k=k: yb.at[k, m],
+                lambda m, k=k: yqr.at[k, m],
+            )
+        )
+        ysum[-1].first()
 
     def chunk(n):
         start = pl.multiple_of(yn[n] * 512, 512)
@@ -258,9 +307,6 @@
 
     gv.from_partner(0)
     pt = chunk(0)
-    rv.step()
-    for k in range(4):
-        gv.y_last(k)
     gv.from_partner(1)
     pt += chunk(1)
     gv.from_partner(2)
@@ -268,45 +314,44 @@
     gv.from_partner(3)
     pt += chunk(3)
     part[...] = pt.T
-
-    def piece(k, h):
-        return rows(part, mod4(x + k) * 128 + 64 * h, 64)
-
-    send(piece(2, 0), ra, rsr.at[0], at_x(1))
-    send(piece(2, 1), rb, rsr.at[1], at_x(3))
-    send(piece(1, 1), fbm, rsr.at[2], at_x(1))
-    send(piece(3, 0), fap, rsr.at[3], at_x(3))
-
-    rv.last()
+    xsum = Sum(
+        at_x,
+        lambda m, h: rows(part, mod4(x + m) * 128 + 64 * h, 64),
+        lambda m: xb.at[m],
+        lambda m: rsr.at[m],
+    )
+    xsum.first()
+    ysum[0].second()
+    ysum[1].second()
+
     sp_[...] = dot3(split(vj[...].T), split(part[...]))
     own = gv.blk(y, zl, c)[...]
     sp_[128:256, 0:128] = dot3(split(own[:, :128].T), split(own[:, 128:]))
     send(rows(sp_, 128 * (1 - c), 128), s1, s1r, partner)
+    ysum[2].second()
+    ysum[3].second()
     arrived(s1, s1r)
     s128[...] = rows(sp_, 128 * c, 128)[...] + s1[...]
     for k in (1, 2, 3):
         send(rows(s128, 32 * mod4(x + k), 32), sx.at[k - 1], sxr.at[k - 1], at_x(k))
-
-    arrived(ra, rsr.at[0])
-    ta[...] = ra[...] + piece(1, 0)[...]
-    send(ta, fam, rsr.at[4], at_x(1))
-    arrived(rb, rsr.at[1])
-    tb[...] = rb[...] + piece(3, 1)[...]
-    send(tb, fbp, rsr.at[5], at_x(3))
+    xsum.second()
+
+    for m, k in enumerate((3, 2, 1, 0)):
+        ysum[m].last(lambda h, k=k: qz.at[k, pl.ds(32 * h, 32)])
+        if k:
+            send(qz.at[k], zb.at[k - 1], zqr.at[k - 1], at_zl(k))
     for k in range(3):
         arrived(sx.at[k], sxr.at[k])
     s32[...] = rows(s128, 32 * x, 32)[...] + sx[0] + (sx[1] + sx[2])
     for k in (1, 2, 3):
         send(rows(s32, 8 * mod4(y + k), 8), sy.at[k - 1], syr.at[k - 1], at_y(k))
-    arrived(fap, rsr.at[3])
-    arrived(fbm, rsr.at[2])
-    arrived(fam, rsr.at[4])
-    total[0:64, :] = piece(0, 0)[...] + (fam[...] + fap[...])
-    send_or_keep(total.at[pl.ds(0, 64)], l1.at[zh], l1r.at[zh], owner(0))
-    arrived(fbp, rsr.at[5])
-    total[64:128, :] = piece(0, 1)[...] + (fbp[...] + fbm[...])
-    send_or_keep(total.at[pl.ds(64, 64)], l1.at[zh], l1r.at[zh], owner(1))
+    xsum.last(lambda h: total.at[pl.ds(64 * h, 64)])
     send(total, hx, hr, at_z(4))
+    for k in range(3):
+        arrived(zb.at[k], zqr.at[k])
+    gp = Gather(1, pi, place)
+    gp.blk(y, zl, c)[...] = (qz[0] + zb[0]) + (zb[1] + zb[2])
+    gp.start()
 
     for k in range(3):
         arrived(sy.at[k], syr.at[k])
@@ -317,21 +362,18 @@
     rp = Ring(1, pj)
     rows(pj, x * 128, 128)[...] = total[...] + hx[...]
     rp.start()
-    for h in range(2):
-        arrived(l1.at[h], l1r.at[h])
-    gp = Gather(1, pi, lambda y_, zl_, c_: (zl_ * 4 + y_) * 2 + c_)
-    gp.blk(y, zl, c)[...] = l1[0] + l1[1]
-    gp.start()
 
     def srow(x_, y_, c_):
         return rows(sfull, 128 * c_ + 32 * x_ + 8 * y_, 8)
 
+    gp.z_step(1)
     for k in range(7):
         arrived(sz.at[k], szr.at[k])
     srow(x, y, c)[...] = s8[...] + sz[0] + (sz[1] + sz[2]) + ((sz[3] + sz[4]) + (sz[5] + sz[6]))
     for k in (1, 2, 3):
         send(srow(x, y, c), srow(x, y, c), s4r.at[k - 1], at_y(k))
-    gp.z_step(1)
+    gp.z_step(2)
+    gp.z_step(3)
     rp.step()
     for k in (1, 2, 3):
         arrived(srow(x, mod4(y - k), c), s4r.at[k - 1])
@@ -339,8 +381,6 @@
     for k in (1, 2, 3):
         send(s_own, s_own, s5r.at[k - 1], at_x(k))
     send(s_own, s_own, s6r.at[0], partner)
-    gp.z_step(2)
-    gp.z_step(3)
     gp.y_step(0)
     for k in (1, 2, 3):
         s_k = rows(sfull, 128 * c + 32 * mod4(x - k), 32)
@@ -380,7 +420,6 @@
     mm = jnp.concatenate(
         [jnp.concatenate([t1, m12], axis=1), jnp.concatenate([zero, t2], axis=1)], axis=0
     )
-    v_s = split(vj[...])
     xj = dot3(split(pj[...]), split(mm)) + dot3(v_s, split(kk))
     zj = dot3(v_s, split(mm.T))
     zh_out[...], zl_out[...] = split(zj.T)
@@ -417,13 +456,13 @@
         out_specs=(pl.BlockSpec(memory_space=pltpu.VMEM),) * 4,
         scratch_shapes=[
             vmem(2048, 512), vmem(2048, 256), vmem(512, 256), vmem(512, 256), vmem(512, 256),
-            vmem(64, 256), vmem(64, 256), vmem(64, 256), vmem(64, 256),
-            vmem(64, 256), vmem(64, 256), vmem(64, 256), vmem(64, 256), vmem(128, 256),
-            vmem(2, 64, 256), vmem(128, 256),
+            vmem(8, 64, 256), vmem(128, 256), vmem(128, 256),
+            vmem(2048, 256), vmem(2048, 256), vmem(4, 8, 32, 256), vmem(4, 64, 256), vmem(3, 64, 256),
             vmem(256, 256), vmem(128, 256), vmem(128, 256), vmem(3, 32, 256), vmem(32, 256),
             vmem(3, 8, 256), vmem(8, 256), vmem(7, 8, 256), vmem(256, 256), vmem(2, 128, 128),
-            dma(160), dma(4), dma(2, 3), dma(2, 4, 4), dma(2, 4, 4), dma(2), dma(2, 4),
-            dma(6), dma(2), dma(), dma(), dma(3), dma(3), dma(7), dma(3), dma(3), dma(4),
+            dma(190), dma(4), dma(2, 3), dma(2, 4, 4), dma(2, 4, 4), dma(2), dma(2, 4),
+            dma(6), dma(), dma(4, 4), dma(4, 6), dma(3),
+            dma(), dma(3), dma(3), dma(7), dma(3), dma(3), dma(4),
         ],
         compiler_params=pltpu.CompilerParams(
             collective_id=0, has_side_effects=True, vmem_limit_bytes=36 << 20

time: 81.6 us -> 89.9 us (1.10)
  Pallas kernels: 81.5 us -> 89.8 us
    pallas_call x1, Pallas kernels: 77.7 us -> 86.1 us  [exchange(): pl.pallas_call(exchange_kernel, out_shape=(jax.ShapeDtypeStruct((2048, 51...]
where the time goes in v3:
time: 89.9 us; the launch traced here: 89.8 us
  Pallas kernels  89.8 us (100%)
    pallas_call x1, Pallas kernels, exchange(): pl.pallas_call(exchange_kernel, out_shape=(jax.ShapeDtypeStruct((2048, 51...  86.1 us
    pallas_call x1, Pallas kernels, update(): pl.pallas_call(update_kernel, grid=(rows_here // step,), out_shape=jax.Sh...  3.76 us

profile of v3, /device:TPU:1, one launch (start us, length us, event | category | flops | bytes accessed | tf_op | source)
XLA Modules:
  0.0 89.8 jit_solution(16812163771158363613)
XLA Ops:
  0.0 86.1 %shard_map.37 = (f32[2048,512]{1,0:T(8,128)S(1)}, f32[2048,256]{1,0:T(8,128)S(1)}, bf16[256,512]{1,0:T(8,128)(2,1)S(1)}, bf16[256,512]{1,0:T(8,128)(2,1)S(1)}) custom-call(f32[2048,512]{1,0:T(8,128)} %mat.1, f32[2,64,128]{2,1,0:T(8,128)} %vec.1, f32[2,128,128]{2,1,0:T(8,128)} %tf.1), custom_call_target="tpu_custom_call" | custom-call | tf_op jit(solution)/shard_map/pallas_call | solution.py:447
  86.1 3.8 %shard_map.38 = f32[2048,512]{1,0:T(8,128)} custom-call(f32[2048,512]{1,0:T(8,128)S(1)} %get-tuple-element.9.mat, f32[2048,256]{1,0:T(8,128)S(1)} %get-tuple-element.10.pi, bf16[256,512]{1,0:T(8,128)(2,1)S(1)} %get-tuple-element.11.zh, bf16[256,512]{1,0:T(8,128)(2,1)S(1)} %get-tuple-element.12.zl), custom_call_target="tpu_custom_call" | custom-call | tf_op jit(solution)/shard_map/pallas_call | solution.py:480

commit v4 on v2

--- a/solution.py
+++ b/solution.py
@@ -27,14 +27,12 @@
 
 
 def dot_full(left, right):
-    return jnp.dot(
-        left, right, precision=lax.Precision.HIGHEST, preferred_element_type=F32
-    )
+    return dot3(split(left), split(right))
 
 
 def exchange_kernel(
     mat, vec, tf, a2, pi, zh_out, zl_out,
-    a, vi, vj, pj, part, ra, rb, ta, tb, fam, fap, fbp, fbm, total, l1, hx,
+    a, vi, vj, pj, part, xb, total, hx,
     sp_, s1, s128, sx, s32, sy, s8, sz, sfull, tfv,
     send_sem, load_sem, zr, yr, cr, l2r, xr, rsr, l1r, hr, s1r, sxr, syr, szr, s4r, s5r, s6r,
 ):
@@ -56,7 +54,8 @@
     def at_y(k):
         return dev(x, zh, mod4(y + k), zl, c)
 
-    zk = [zl, zl + 1 - 2 * lax.rem(zl, 2), mod4(zl + 2), 3 - zl]
+    zk = [zl, zl + 1 - 2 * lax.rem(zl, 2), 2 - lax.div(zl, 2), 3 - 3 * lax.div(zl, 2)]
+    middle = jnp.logical_and(zl > 0, zl < 3)
     yn = [y, mod4(y - 1), mod4(y + 1), mod4(y + 2)]
 
     def at_zl(k):
@@ -72,11 +71,8 @@
     def spread_from(h):
         return dev(y, lax.div(zl, 2), lax.rem(zl, 2) * 2 + c, x, h)
 
-    def owner(h):
-        return dev(y, lax.div(zl, 2), x, lax.rem(zl, 2) * 2 + c, h)
-
-    def owned_from(h):
-        return dev(y, h, x, 2 * zh + lax.div(zl, 2), lax.rem(zl, 2))
+    owner = dev(y, lax.div(zl, 2), x, 2 * zh + lax.rem(zl, 2), c)
+    owned_from = dev(y, lax.div(zl, 2), x, 2 * zh + lax.rem(zl, 2), c)
 
     def is_me(d):
         return jnp.logical_and(d[0] == row, d[1] == col)
@@ -86,13 +82,20 @@
 
     sent = []
 
-    def send(src, dst, sem, device):
+    def send(src, dst, sem, device, when=None):
         copy = pltpu.make_async_remote_copy(
             src_ref=src, dst_ref=dst, send_sem=send_sem.at[len(sent)], recv_sem=sem,
             device_id=device, device_id_type=MESH,
         )
-        copy.start()
-        sent.append((copy, None))
+        if when is None:
+            copy.start()
+        else:
+
+            @pl.when(when)
+            def _():
+                copy.start()
+
+        sent.append((copy, when))
 
     def send_or_keep(src, dst, sem, device):
         mine = is_me(device)
@@ -145,7 +148,7 @@
     peers += [at_z(k) for k in range(1, 8)]
     for peer in peers:
         pl.semaphore_signal(barrier, inc=1, device_id=peer, device_id_type=MESH)
-    others = [f(h) for f in (spread_to, spread_from, owner, owned_from) for h in range(2)]
+    others = [f(h) for f in (spread_to, spread_from) for h in range(2)] + [owner, owned_from]
     for peer in others:
 
         @pl.when(jnp.logical_not(is_me(peer)))
@@ -174,35 +177,44 @@
             send(b, b, cr.at[self.n, n, k], partner)
 
         def to_y(self, k):
-            b = self.blk(y, zk[k], c)
-            send(b, b, yr.at[self.n, k, 0], at_y(1))
-            send(b, b, yr.at[self.n, k, 1], at_y(3))
+            for h, s in ((0, 0), (1, 1)):
+                b = self.half(y, zk[k], c, h)
+                send(b, b, yr.at[self.n, k, s], at_y(1))
+            for h, s in ((1, 2), (0, 3)):
+                b = self.half(y, zk[k], c, h)
+                send(b, b, yr.at[self.n, k, s], at_y(3))
+
+        def to_z(self, k, n, h, when):
+            b = self.half(y, zk[k], c, h)
+            sem = {(0, 1): 0, (0, 2): 1, (1, 2): 2, (2, 1): 1, (3, 1): 2}[k, n]
+            send(b, b, zr.at[self.n, sem, h], at_zl(n), when)
 
         def start(self):
-            b = self.blk(y, zl, c)
-            for k in (1, 2, 3):
-                send(b, b, zr.at[self.n, k - 1], at_zl(k))
+            for h in range(2):
+                self.to_z(0, 1, h, None)
+                self.to_z(0, 2, h, middle)
             self.to_y(0)
             self.to_partner(0, 0)
 
         def z_step(self, k):
-            arrived(self.blk(y, zk[k], c), zr.at[self.n, k - 1])
+            for h in range(2):
+                arrived(self.half(y, zk[k], c, h), zr.at[self.n, k - 1, h])
+                self.to_z(k, 2 if k == 1 else 1, h, middle)
             self.to_y(k)
             self.to_partner(0, k)
 
         def y_step(self, k):
-            arrived(self.blk(yn[1], zk[k], c), yr.at[self.n, k, 0])
-            h = self.half(yn[1], zk[k], c, 0)
-            send(h, h, yr.at[self.n, k, 2], at_y(1))
-            self.to_partner(1, k)
-            arrived(self.blk(yn[2], zk[k], c), yr.at[self.n, k, 1])
-            h = self.half(yn[2], zk[k], c, 1)
-            send(h, h, yr.at[self.n, k, 3], at_y(3))
-            self.to_partner(2, k)
+            for n, h, s, to in ((1, 0, 0, 1), (2, 1, 2, 3)):
+                b = self.half(yn[n], zk[k], c, h)
+                arrived(b, yr.at[self.n, k, s])
+                send(b, b, yr.at[self.n, k, 4 + h], at_y(to))
+            for n, h, s in ((1, 1, 1), (2, 0, 3)):
+                arrived(self.half(yn[n], zk[k], c, h), yr.at[self.n, k, s])
+                self.to_partner(n, k)
 
         def y_last(self, k):
             for h in range(2):
-                arrived(self.half(yn[3], zk[k], c, h), yr.at[self.n, k, 2 + h])
+                arrived(self.half(yn[3], zk[k], c, h), yr.at[self.n, k, 4 + h])
             self.to_partner(3, k)
 
         def from_partner(self, n):
@@ -213,25 +225,45 @@
         def __init__(self, n, small):
             self.n, self.small = n, small
 
+        def half(self, k, h):
+            return rows(self.small, mod4(x + k) * 128 + 64 * h, 64)
+
         def start(self):
-            b = rows(self.small, x * 128, 128)
-            send(b, b, xr.at[self.n, 0], at_x(1))
-            send(b, b, xr.at[self.n, 1], at_x(3))
+            for h, s, to in ((0, 0, 1), (1, 2, 3), (1, 1, 1), (0, 3, 3)):
+                b = self.half(0, h)
+                send(b, b, xr.at[self.n, s], at_x(to))
 
         def step(self):
-            m = mod4(x - 1)
-            arrived(rows(self.small, m * 128, 128), xr.at[self.n, 0])
-            h = rows(self.small, m * 128, 64)
-            send(h, h, xr.at[self.n, 2], at_x(1))
-            m = mod4(x + 1)
-            arrived(rows(self.small, m * 128, 128), xr.at[self.n, 1])
-            h = rows(self.small, m * 128 + 64, 64)
-            send(h, h, xr.at[self.n, 3], at_x(3))
+            for k, h, s, to in ((-1, 0, 0, 1), (1, 1, 2, 3)):
+                b = self.half(k, h)
+                arrived(b, xr.at[self.n, s])
+                send(b, b, xr.at[self.n, 4 + h], at_x(to))
 
         def last(self):
-            m = mod4(x + 2)
+            for k, h, s in ((-1, 1, 1), (1, 0, 3), (2, 0, 4), (2, 1, 5)):
+                arrived(self.half(k, h), xr.at[self.n, s])
+
+    class Sum:
+        def __init__(self, at, piece, buf, sem):
+            self.at, self.piece, self.buf, self.sem = at, piece, buf, sem
+
+        def first(self):
+            send(self.piece(2, 0), self.buf(0), self.sem(0), self.at(1))
+            send(self.piece(2, 1), self.buf(1), self.sem(1), self.at(3))
+            send(self.piece(1, 1), self.buf(2), self.sem(2), self.at(1))
+            send(self.piece(3, 0), self.buf(3), self.sem(3), self.at(3))
+
+        def second(self):
+            for h, k, to in ((0, 1, 1), (1, 3, 3)):
+                arrived(self.buf(h), self.sem(h))
+                self.buf(6 + h)[...] = self.buf(h)[...] + self.piece(k, h)[...]
+                send(self.buf(6 + h), self.buf(4 + h), self.sem(4 + h), self.at(to))
+
+        def last(self, out):
             for h in range(2):
-                arrived(rows(self.small, m * 128 + 64 * h, 64), xr.at[self.n, 2 + h])
+                arrived(self.buf(3 - h), self.sem(3 - h))
+                arrived(self.buf(4 + h), self.sem(4 + h))
+                out(h)[...] = self.piece(0, h)[...] + (self.buf(4 + h)[...] + self.buf(3 - h)[...])
 
     gv = Gather(0, vi, lambda y_, zl_, c_: (y_ * 4 + zl_) * 2 + c_)
     rv = Ring(0, vj)
@@ -269,59 +301,45 @@
     pt += chunk(3)
     part[...] = pt.T
 
-    def piece(k, h):
-        return rows(part, mod4(x + k) * 128 + 64 * h, 64)
-
-    send(piece(2, 0), ra, rsr.at[0], at_x(1))
-    send(piece(2, 1), rb, rsr.at[1], at_x(3))
-    send(piece(1, 1), fbm, rsr.at[2], at_x(1))
-    send(piece(3, 0), fap, rsr.at[3], at_x(3))
+    xsum = Sum(
+        at_x,
+        lambda m, h: rows(part, mod4(x + m) * 128 + 64 * h, 64),
+        lambda m: xb.at[m],
+        lambda m: rsr.at[m],
+    )
+    xsum.first()
 
     rv.last()
     sp_[...] = dot3(split(vj[...].T), split(part[...]))
     own = gv.blk(y, zl, c)[...]
     sp_[128:256, 0:128] = dot3(split(own[:, :128].T), split(own[:, 128:]))
     send(rows(sp_, 128 * (1 - c), 128), s1, s1r, partner)
+    xsum.second()
     arrived(s1, s1r)
     s128[...] = rows(sp_, 128 * c, 128)[...] + s1[...]
     for k in (1, 2, 3):
         send(rows(s128, 32 * mod4(x + k), 32), sx.at[k - 1], sxr.at[k - 1], at_x(k))
 
-    arrived(ra, rsr.at[0])
-    ta[...] = ra[...] + piece(1, 0)[...]
-    send(ta, fam, rsr.at[4], at_x(1))
-    arrived(rb, rsr.at[1])
-    tb[...] = rb[...] + piece(3, 1)[...]
-    send(tb, fbp, rsr.at[5], at_x(3))
+    xsum.last(lambda h: total.at[pl.ds(64 * h, 64)])
+    send(rows(total, 64 * (1 - zh), 64), hx, hr.at[0], at_z(4))
     for k in range(3):
         arrived(sx.at[k], sxr.at[k])
     s32[...] = rows(s128, 32 * x, 32)[...] + sx[0] + (sx[1] + sx[2])
     for k in (1, 2, 3):
         send(rows(s32, 8 * mod4(y + k), 8), sy.at[k - 1], syr.at[k - 1], at_y(k))
-    arrived(fap, rsr.at[3])
-    arrived(fbm, rsr.at[2])
-    arrived(fam, rsr.at[4])
-    total[0:64, :] = piece(0, 0)[...] + (fam[...] + fap[...])
-    send_or_keep(total.at[pl.ds(0, 64)], l1.at[zh], l1r.at[zh], owner(0))
-    arrived(fbp, rsr.at[5])
-    total[64:128, :] = piece(0, 1)[...] + (fbp[...] + fbm[...])
-    send_or_keep(total.at[pl.ds(64, 64)], l1.at[zh], l1r.at[zh], owner(1))
-    send(total, hx, hr, at_z(4))
-
     for k in range(3):
         arrived(sy.at[k], syr.at[k])
     s8[...] = rows(s32, 8 * y, 8)[...] + sy[0] + (sy[1] + sy[2])
     for k in range(1, 8):
         send(s8, sz.at[k - 1], szr.at[k - 1], at_z(k))
-    arrived(hx, hr)
-    rp = Ring(1, pj)
-    rows(pj, x * 128, 128)[...] = total[...] + hx[...]
-    rp.start()
-    for h in range(2):
-        arrived(l1.at[h], l1r.at[h])
-    gp = Gather(1, pi, lambda y_, zl_, c_: (zl_ * 4 + y_) * 2 + c_)
-    gp.blk(y, zl, c)[...] = l1[0] + l1[1]
-    gp.start()
+    arrived(hx, hr.at[0])
+    p_own = rows(pj, x * 128 + 64 * zh, 64)
+    p_own[...] = rows(total, 64 * zh, 64)[...] + hx[...]
+    gp = Gather(
+        1, pi, lambda y_, zl_, c_: (lax.rem(zl_, 2) * 2 + c_) * 8 + 2 * y_ + lax.div(zl_, 2)
+    )
+    send_or_keep(p_own, gp.blk(x, 2 * zh + lax.rem(zl, 2), c), l1r, owner)
+    send(p_own, p_own, hr.at[1], at_z(4))
 
     def srow(x_, y_, c_):
         return rows(sfull, 128 * c_ + 32 * x_ + 8 * y_, 8)
@@ -331,23 +349,24 @@
     srow(x, y, c)[...] = s8[...] + sz[0] + (sz[1] + sz[2]) + ((sz[3] + sz[4]) + (sz[5] + sz[6]))
     for k in (1, 2, 3):
         send(srow(x, y, c), srow(x, y, c), s4r.at[k - 1], at_y(k))
-    gp.z_step(1)
-    rp.step()
+    arrived(gp.blk(y, zl, c), l1r)
+    gp.start()
     for k in (1, 2, 3):
         arrived(srow(x, mod4(y - k), c), s4r.at[k - 1])
     s_own = rows(sfull, 128 * c + 32 * x, 32)
     for k in (1, 2, 3):
         send(s_own, s_own, s5r.at[k - 1], at_x(k))
     send(s_own, s_own, s6r.at[0], partner)
-    gp.z_step(2)
-    gp.z_step(3)
-    gp.y_step(0)
+    rp = Ring(1, pj)
+    arrived(rows(pj, x * 128 + 64 * (1 - zh), 64), hr.at[1])
+    rp.start()
+    gp.z_step(1)
     for k in (1, 2, 3):
         s_k = rows(sfull, 128 * c + 32 * mod4(x - k), 32)
         arrived(s_k, s5r.at[k - 1])
         send(s_k, s_k, s6r.at[k], partner)
-    rp.last()
-    gp.y_step(1)
+    gp.z_step(2)
+    gp.z_step(3)
     for k in range(4):
         arrived(rows(sfull, 128 * (1 - c) + 32 * mod4(x - k), 32), s6r.at[k])
 
@@ -361,14 +380,16 @@
     t1t, t2t = t1.T, t2.T
     b = dot_full(t1t, dot_full(s11, t1))
     e = dot_full(t1t, s12)
+    nt2 = dot_full(n12, t2)
+    gp.y_step(0)
+    rp.step()
     h = dot_full(b.T, n12)
-    gp.y_step(2)
-    nt2 = dot_full(n12, t2)
-    f = dot_full(n12.T, e - 0.5 * h)
     k12 = dot_full(h - e, t2)
     m12 = -dot_full(t1, nt2)
+    f = dot_full(n12.T, e - 0.5 * h)
+    gp.y_step(1)
     b2 = dot_full(t2t, dot_full(s22 - f - f.T, t2))
-    gp.y_step(3)
+    gp.y_step(2)
     zero = jnp.zeros((128, 128), F32)
     kk = jnp.concatenate(
         [
@@ -380,19 +401,19 @@
     mm = jnp.concatenate(
         [jnp.concatenate([t1, m12], axis=1), jnp.concatenate([zero, t2], axis=1)], axis=0
     )
+    rp.last()
     v_s = split(vj[...])
     xj = dot3(split(pj[...]), split(mm)) + dot3(v_s, split(kk))
+    x_s = split(xj.T)
+    gp.y_step(3)
     zj = dot3(v_s, split(mm.T))
     zh_out[...], zl_out[...] = split(zj.T)
-    x_s = split(xj.T)
-    gp.y_last(0)
-    gp.y_last(1)
     for n in range(4):
+        if n == 2:
+            for k in range(4):
+                gp.y_last(k)
         r = slice(512 * n, 512 * n + 512)
         a2[r, :] = a[r, :] - dot3(split(vi[r, :]), x_s)
-        if n == 0:
-            gp.y_last(2)
-            gp.y_last(3)
     for n in range(4):
         gp.from_partner(n)
     finish()
@@ -417,13 +438,11 @@
         out_specs=(pl.BlockSpec(memory_space=pltpu.VMEM),) * 4,
         scratch_shapes=[
             vmem(2048, 512), vmem(2048, 256), vmem(512, 256), vmem(512, 256), vmem(512, 256),
-            vmem(64, 256), vmem(64, 256), vmem(64, 256), vmem(64, 256),
-            vmem(64, 256), vmem(64, 256), vmem(64, 256), vmem(64, 256), vmem(128, 256),
-            vmem(2, 64, 256), vmem(128, 256),
+            vmem(8, 64, 256), vmem(128, 256), vmem(64, 256),
             vmem(256, 256), vmem(128, 256), vmem(128, 256), vmem(3, 32, 256), vmem(32, 256),
             vmem(3, 8, 256), vmem(8, 256), vmem(7, 8, 256), vmem(256, 256), vmem(2, 128, 128),
-            dma(160), dma(4), dma(2, 3), dma(2, 4, 4), dma(2, 4, 4), dma(2), dma(2, 4),
-            dma(6), dma(2), dma(), dma(), dma(3), dma(3), dma(7), dma(3), dma(3), dma(4),
+            dma(160), dma(4), dma(2, 3, 2), dma(2, 4, 6), dma(2, 4, 4), dma(2), dma(2, 6),
+            dma(6), dma(), dma(2), dma(), dma(3), dma(3), dma(7), dma(3), dma(3), dma(4),
         ],
         compiler_params=pltpu.CompilerParams(
             collective_id=0, has_side_effects=True, vmem_limit_bytes=36 << 20

time: 81.6 us -> 78.3 us (0.960)
  Pallas kernels: 81.5 us -> 78.2 us
    pallas_call x1, Pallas kernels: 77.7 us -> 74.5 us  [exchange(): pl.pallas_call(exchange_kernel, out_shape=(jax.ShapeDtypeStruct((2048, 51...]
where the time goes in v4:
time: 78.3 us; the launch traced here: 78.2 us
  Pallas kernels  78.2 us (100%)
    pallas_call x1, Pallas kernels, exchange(): pl.pallas_call(exchange_kernel, out_shape=(jax.ShapeDtypeStruct((2048, 51...  74.5 us
    pallas_call x1, Pallas kernels, update(): pl.pallas_call(update_kernel, grid=(rows_here // step,), out_shape=jax.Sh...  3.74 us

profile of v4, /device:TPU:1, one launch (start us, length us, event | category | flops | bytes accessed | tf_op | source)
XLA Modules:
  0.0 78.2 jit_solution(1274794818531842154)
XLA Ops:
  0.0 74.5 %shard_map.37 = (f32[2048,512]{1,0:T(8,128)S(1)}, f32[2048,256]{1,0:T(8,128)S(1)}, bf16[256,512]{1,0:T(8,128)(2,1)S(1)}, bf16[256,512]{1,0:T(8,128)(2,1)S(1)}) custom-call(f32[2048,512]{1,0:T(8,128)} %mat.1, f32[2,64,128]{2,1,0:T(8,128)} %vec.1, f32[2,128,128]{2,1,0:T(8,128)} %tf.1), custom_call_target="tpu_custom_call" | custom-call | tf_op jit(solution)/shard_map/pallas_call | solution.py:429
  74.5 3.7 %shard_map.38 = f32[2048,512]{1,0:T(8,128)} custom-call(f32[2048,512]{1,0:T(8,128)S(1)} %get-tuple-element.9.mat, f32[2048,256]{1,0:T(8,128)S(1)} %get-tuple-element.10.pi, bf16[256,512]{1,0:T(8,128)(2,1)S(1)} %get-tuple-element.11.zh, bf16[256,512]{1,0:T(8,128)(2,1)S(1)} %get-tuple-element.12.zl), custom_call_target="tpu_custom_call" | custom-call | tf_op jit(solution)/shard_map/pallas_call | solution.py:460

commit v5 on v4

--- a/solution.py
+++ b/solution.py
@@ -9,6 +9,7 @@
 F32 = jnp.float32
 BF16 = jnp.bfloat16
 NN = ((1,), (0,))
+DIRECT = (3,)
 TN = ((0,), (0,))
 
 
@@ -177,6 +178,11 @@
             send(b, b, cr.at[self.n, n, k], partner)
 
         def to_y(self, k):
+            if k in DIRECT:
+                b = self.blk(y, zk[k], c)
+                for s, n in ((0, 1), (2, 3), (4, 2)):
+                    send(b, b, yr.at[self.n, k, s], at_y(n))
+                return
             for h, s in ((0, 0), (1, 1)):
                 b = self.half(y, zk[k], c, h)
                 send(b, b, yr.at[self.n, k, s], at_y(1))
@@ -204,6 +210,11 @@
             self.to_partner(0, k)
 
         def y_step(self, k):
+            if k in DIRECT:
+                for n, s in ((1, 0), (2, 2)):
+                    arrived(self.blk(yn[n], zk[k], c), yr.at[self.n, k, s])
+                    self.to_partner(n, k)
+                return
             for n, h, s, to in ((1, 0, 0, 1), (2, 1, 2, 3)):
                 b = self.half(yn[n], zk[k], c, h)
                 arrived(b, yr.at[self.n, k, s])
@@ -213,6 +224,10 @@
                 self.to_partner(n, k)
 
         def y_last(self, k):
+            if k in DIRECT:
+                arrived(self.blk(yn[3], zk[k], c), yr.at[self.n, k, 4])
+                self.to_partner(3, k)
+                return
             for h in range(2):
                 arrived(self.half(yn[3], zk[k], c, h), yr.at[self.n, k, 4 + h])
             self.to_partner(3, k)
@@ -225,23 +240,16 @@
         def __init__(self, n, small):
             self.n, self.small = n, small
 
-        def half(self, k, h):
-            return rows(self.small, mod4(x + k) * 128 + 64 * h, 64)
+        def own(self, k):
+            return rows(self.small, mod4(x + k) * 128, 128)
 
         def start(self):
-            for h, s, to in ((0, 0, 1), (1, 2, 3), (1, 1, 1), (0, 3, 3)):
-                b = self.half(0, h)
-                send(b, b, xr.at[self.n, s], at_x(to))
-
-        def step(self):
-            for k, h, s, to in ((-1, 0, 0, 1), (1, 1, 2, 3)):
-                b = self.half(k, h)
-                arrived(b, xr.at[self.n, s])
-                send(b, b, xr.at[self.n, 4 + h], at_x(to))
+            for k in (1, 3, 2):
+                send(self.own(0), self.own(0), xr.at[self.n, k - 1], at_x(k))
 
         def last(self):
-            for k, h, s in ((-1, 1, 1), (1, 0, 3), (2, 0, 4), (2, 1, 5)):
-                arrived(self.half(k, h), xr.at[self.n, s])
+            for k in (1, 3, 2):
+                arrived(self.own(-k), xr.at[self.n, k - 1])
 
     class Sum:
         def __init__(self, at, piece, buf, sem):
@@ -290,7 +298,6 @@
 
     gv.from_partner(0)
     pt = chunk(0)
-    rv.step()
     for k in range(4):
         gv.y_last(k)
     gv.from_partner(1)
@@ -382,7 +389,6 @@
     e = dot_full(t1t, s12)
     nt2 = dot_full(n12, t2)
     gp.y_step(0)
-    rp.step()
     h = dot_full(b.T, n12)
     k12 = dot_full(h - e, t2)
     m12 = -dot_full(t1, nt2)
@@ -456,7 +462,7 @@
 
 def update(matrix, pi, zh, zl):
     rows_here, cols_here = matrix.shape
-    step = 512
+    step = 1024
     return pl.pallas_call(
         update_kernel,
         grid=(rows_here // step,),

time: 78.3 us -> 76 us (0.971)
  Pallas kernels: 78.2 us -> 75.9 us
    pallas_call x1, Pallas kernels: 74.5 us -> 72.6 us  [exchange(): pl.pallas_call(exchange_kernel, out_shape=(jax.ShapeDtypeStruct((2048, 51...]
where the time goes in v5:
time: 76 us
  Pallas kernels  75.9 us (100%)
    pallas_call x1, Pallas kernels, exchange(): pl.pallas_call(exchange_kernel, out_shape=(jax.ShapeDtypeStruct((2048, 51...  72.6 us
    pallas_call x1, Pallas kernels, update(): pl.pallas_call(update_kernel, grid=(rows_here // step,), out_shape=jax.Sh...  3.32 us

profile of v5, /device:TPU:1, one launch (start us, length us, event | category | flops | bytes accessed | tf_op | source)
XLA Modules:
  0.0 76.0 jit_solution(11682284686198344556)
XLA Ops:
  0.0 72.6 %shard_map.37 = (f32[2048,512]{1,0:T(8,128)S(1)}, f32[2048,256]{1,0:T(8,128)S(1)}, bf16[256,512]{1,0:T(8,128)(2,1)S(1)}, bf16[256,512]{1,0:T(8,128)(2,1)S(1)}) custom-call(f32[2048,512]{1,0:T(8,128)} %mat.1, f32[2,64,128]{2,1,0:T(8,128)} %vec.1, f32[2,128,128]{2,1,0:T(8,128)} %tf.1), custom_call_target="tpu_custom_call" | custom-call | tf_op jit(solution)/shard_map/pallas_call | solution.py:435
  72.6 3.3 %shard_map.38 = f32[2048,512]{1,0:T(8,128)} custom-call(f32[2048,512]{1,0:T(8,128)S(1)} %get-tuple-element.9.mat, f32[2048,256]{1,0:T(8,128)S(1)} %get-tuple-element.10.pi, bf16[256,512]{1,0:T(8,128)(2,1)S(1)} %get-tuple-element.11.zh, bf16[256,512]{1,0:T(8,128)(2,1)S(1)} %get-tuple-element.12.zl), custom_call_target="tpu_custom_call" | custom-call | tf_op jit(solution)/shard_map/pallas_call | solution.py:466

commit v6 on v5

--- a/solution.py
+++ b/solution.py
@@ -368,12 +368,13 @@
     arrived(rows(pj, x * 128 + 64 * (1 - zh), 64), hr.at[1])
     rp.start()
     gp.z_step(1)
+    gp.z_step(2)
+    gp.z_step(3)
     for k in (1, 2, 3):
         s_k = rows(sfull, 128 * c + 32 * mod4(x - k), 32)
         arrived(s_k, s5r.at[k - 1])
         send(s_k, s_k, s6r.at[k], partner)
-    gp.z_step(2)
-    gp.z_step(3)
+    gp.y_step(0)
     for k in range(4):
         arrived(rows(sfull, 128 * (1 - c) + 32 * mod4(x - k), 32), s6r.at[k])
 
@@ -388,14 +389,13 @@
     b = dot_full(t1t, dot_full(s11, t1))
     e = dot_full(t1t, s12)
     nt2 = dot_full(n12, t2)
-    gp.y_step(0)
+    gp.y_step(1)
     h = dot_full(b.T, n12)
     k12 = dot_full(h - e, t2)
     m12 = -dot_full(t1, nt2)
     f = dot_full(n12.T, e - 0.5 * h)
-    gp.y_step(1)
+    gp.y_step(2)
     b2 = dot_full(t2t, dot_full(s22 - f - f.T, t2))
-    gp.y_step(2)
     zero = jnp.zeros((128, 128), F32)
     kk = jnp.concatenate(
         [

time: 76 us -> 73.6 us (0.968)
  Pallas kernels: 75.9 us -> 73.5 us
    pallas_call x1, Pallas kernels: 72.6 us -> 70.2 us  [exchange(): pl.pallas_call(exchange_kernel, out_shape=(jax.ShapeDtypeStruct((2048, 51...]
where the time goes in v6:
time: 73.6 us; the launch traced here: 73.5 us
  Pallas kernels  73.5 us (100%)
    pallas_call x1, Pallas kernels, exchange(): pl.pallas_call(exchange_kernel, out_shape=(jax.ShapeDtypeStruct((2048, 51...  70.2 us
    pallas_call x1, Pallas kernels, update(): pl.pallas_call(update_kernel, grid=(rows_here // step,), out_shape=jax.Sh...  3.32 us

profile of v6, /device:TPU:1, one launch (start us, length us, event | category | flops | bytes accessed | tf_op | source)
XLA Modules:
  0.0 73.5 jit_solution(14995309560973875533)
XLA Ops:
  0.0 70.2 %shard_map.37 = (f32[2048,512]{1,0:T(8,128)S(1)}, f32[2048,256]{1,0:T(8,128)S(1)}, bf16[256,512]{1,0:T(8,128)(2,1)S(1)}, bf16[256,512]{1,0:T(8,128)(2,1)S(1)}) custom-call(f32[2048,512]{1,0:T(8,128)} %mat.1, f32[2,64,128]{2,1,0:T(8,128)} %vec.1, f32[2,128,128]{2,1,0:T(8,128)} %tf.1), custom_call_target="tpu_custom_call" | custom-call | tf_op jit(solution)/shard_map/pallas_call | solution.py:435
  70.2 3.3 %shard_map.38 = f32[2048,512]{1,0:T(8,128)} custom-call(f32[2048,512]{1,0:T(8,128)S(1)} %get-tuple-element.9.mat, f32[2048,256]{1,0:T(8,128)S(1)} %get-tuple-element.10.pi, bf16[256,512]{1,0:T(8,128)(2,1)S(1)} %get-tuple-element.11.zh, bf16[256,512]{1,0:T(8,128)(2,1)S(1)} %get-tuple-element.12.zl), custom_call_target="tpu_custom_call" | custom-call | tf_op jit(solution)/shard_map/pallas_call | solution.py:466
